TPU v7x, 32 devices: a whole 2x2x4 slice. The times are simulated.
32 devices in a mesh: groups: 2 (over x), ctx: 16 (over z, y, core).
Axes of the slice: x: 2, y: 2, z: 4, core: 2. Of those that a mesh axis runs over, the one named last changes fastest.
Arguments:
- queries: bfloat16 [256, 8192], P(('groups', 'ctx')), parts along dimension 0, may hold values from -8 to 8
- prefix_key_heads: bfloat16 [16384, 1024], P(('groups', 'ctx')), parts along dimension 0, may hold values from -8 to 8
- prefix_value_heads: bfloat16 [16384, 1024], P(('groups', 'ctx')), parts along dimension 0, may hold values from -6 to 6
- tree_key_heads: bfloat16 [256, 1024], P(('groups', 'ctx')), parts along dimension 0, may hold values from -16 to 16
- tree_value_heads: bfloat16 [256, 1024], P(('groups', 'ctx')), parts along dimension 0, may hold values from -6 to 6
- token_embed: bfloat16 [256, 8192], P(('groups', 'ctx')), parts along dimension 0, may hold values from -12 to 12
- fc_embed: bfloat16 [8192, 8192], P('ctx'), may hold values from -0.25 to 0.25
- fc_feature: bfloat16 [8192, 8192], P('ctx'), may hold values from -0.0625 to 0.0625
- draft_gain: float32 [8192], replicated, may hold values from 0.5 to 1.5
- parents: int32 [4, 64], P('groups'), parts along dimension 0, may hold values from 0 to 62, as said below
- accepted: int32 [4], P('groups'), parts along dimension 0, may hold values from 0 to 63, as said below
Outputs:
- attended: bfloat16 [256, 8192], P(('groups', 'ctx')), parts along dimension 0
- draft_input: bfloat16 [256, 8192], P(('groups', 'ctx')), parts along dimension 0
There are 2 independent parts, one for each index of `groups`. A program takes and returns all parts, laid end to end along the dimension named above; an argument that names none is the same for every part. Nothing has to cross between parts.
Inputs may be any that keep to these rules, and one draw needn't show every extreme that they name: parents[t, 0] = 0 marks the root; every other node's parent is an earlier node of the same tree; no node lies more than 6 steps below its root, and every tree has a node exactly 6 steps below it. The accepted rows of tree t are node accepted[t] and all its ancestors, so at most 7 rows a tree; in every draw some tree accepts exactly 7 rows.
All inputs are finite; a program needn't handle non-finite values.
Results may differ from a plain program's by a relative error of at most 0.0028.
Values may be sent and summed in bfloat16 or wider, within the bound.
No kernel may reach another device: no remote copies, remote signals or barrier semaphores. Data moves between devices by JAX's collectives and lax.ppermute only.
A program may use at most 128 MiB of HBM per device.

v0:
```python
import functools
import math

import jax
import jax.numpy as jnp
from jax import lax
from jax.experimental import pallas as pl
from jax.experimental.pallas import tpu as pltpu
from jax.sharding import PartitionSpec as P


QUERY_HEADS = 64
KEY_HEADS = 8
HEAD_WIDTH = 128
PER_KEY = QUERY_HEADS // KEY_HEADS
SLOTS = 8
LANES = 128
GROUP = KEY_HEADS
HEAD_COLUMNS = PER_KEY * HEAD_WIDTH
WEIGHT_PIECES = 8
ROOM = 14 * 2**20
STEP = 32
ARRIVAL = (0, 2, 4, 3, 5, 6, 7, 1)
NEGATIVE = -1e30
LOG2_SCALE = HEAD_WIDTH**-0.5 * math.log2(math.e)

f32 = jnp.float32
bf16 = jnp.bfloat16


def dot_t(a, b):
    return lax.dot_general(a, b, (((1,), (1,)), ((), ())), preferred_element_type=f32)


def dot(a, b):
    return lax.dot_general(a, b, (((1,), (0,)), ((), ())), preferred_element_type=f32)


def attend(q, slabs, positions, tree_kv, bias):
    scores = [dot_t(q, s[0:positions, 0:HEAD_WIDTH]) for s in slabs]
    scores.append(dot_t(q, tree_kv[:, 0:HEAD_WIDTH]) + bias)
    top = scores[-1].max(axis=1, keepdims=True)
    for s in scores[:-1]:
        top = jnp.maximum(top, s.max(axis=1, keepdims=True))
    den = jnp.zeros_like(top)
    num = jnp.zeros((q.shape[0], HEAD_WIDTH), f32)
    values = [s[0:positions, HEAD_WIDTH : 2 * HEAD_WIDTH] for s in slabs]
    values.append(tree_kv[:, HEAD_WIDTH : 2 * HEAD_WIDTH])
    for s, v in zip(scores, values):
        w = jnp.exp2((s - top) * LOG2_SCALE)
        den = den + w.sum(axis=1, keepdims=True)
        num = num + dot(w.astype(bf16), v)
    return num / den, top * LOG2_SCALE + jnp.log2(den)


def stack_heads(q):
    q = q.astype(f32)
    return jnp.concatenate(
        [q[:, h * HEAD_WIDTH : (h + 1) * HEAD_WIDTH] for h in range(PER_KEY)], axis=0
    ).astype(bf16)


def bulk_kernel(place_ref, mix_ref, *refs, distance, first, plane_rows, positions):
    slabs = refs[:GROUP]
    tree_ref, bias_ref = refs[GROUP : GROUP + 2]
    out_ref = refs[-1]
    step = out_ref.shape[0]
    start = pl.multiple_of((place_ref[0] ^ distance) * plane_rows + first, step)
    q = stack_heads(mix_ref[pl.ds(start, step), 0:HEAD_COLUMNS])
    bias = jnp.concatenate([bias_ref[pl.ds(start, step), :]] * PER_KEY, axis=0)
    out, lse = attend(q, slabs, positions, tree_ref, bias)
    lane = lax.broadcasted_iota(jnp.int32, (step, LANES), 1)
    stats = jnp.zeros((step, LANES), f32)
    for h in range(PER_KEY):
        part = slice(h * step, (h + 1) * step)
        column = slice(h * HEAD_WIDTH, (h + 1) * HEAD_WIDTH)
        out_ref[:, column] = out[part].astype(bf16)
        high = lse[part].astype(bf16).astype(f32)
        middle = (lse[part] - high).astype(bf16).astype(f32)
        low = lse[part] - high - middle
        stats = jnp.where(lane == h, high, stats)
        stats = jnp.where(lane == PER_KEY + h, middle, stats)
        stats = jnp.where(lane == 2 * PER_KEY + h, low, stats)
    out_ref[:, HEAD_COLUMNS : HEAD_COLUMNS + LANES] = stats.astype(bf16)


def accepted_kernel(place_ref, mix_ref, *refs, planes, positions, feat):
    slabs = refs[:GROUP]
    tree_ref, bias_ref, pick_ref = refs[GROUP : GROUP + 3]
    outs = refs[GROUP + 3 : GROUP + 3 + planes]
    hold_ref = refs[GROUP + 3 + planes]
    rows = pick_ref.shape[0]
    q = stack_heads(dot(pick_ref[...], mix_ref[:, 0:HEAD_COLUMNS]))
    bias = jnp.concatenate([bias_ref[...]] * PER_KEY, axis=0)
    out, lse = attend(q, slabs, positions, tree_ref, bias)
    lane = lax.broadcasted_iota(jnp.int32, (rows, LANES), 1)
    stats = [jnp.zeros((rows, LANES), f32) for _ in range(planes)]
    for h in range(PER_KEY):
        chunk, start = h * HEAD_WIDTH // feat, h * HEAD_WIDTH % feat
        part = slice(h * rows, (h + 1) * rows)
        hold_ref[chunk, :, start : start + HEAD_WIDTH] = out[part]
        stats[chunk] = jnp.where(lane == start // HEAD_WIDTH, lse[part], stats[chunk])
    for chunk in range(planes):
        hold_ref[chunk, :, feat : feat + LANES] = stats[chunk]
    for k in range(planes):
        outs[k][...] = hold_ref[place_ref[0] ^ k]


def merge_head(parts, logs):
    top = functools.reduce(jnp.maximum, logs)
    weights = [jnp.exp2(s - top) for s in logs]
    den = functools.reduce(jnp.add, weights)
    num = functools.reduce(jnp.add, [w * p for w, p in zip(weights, parts)])
    return num / den


def merge_kernel(*refs, planes):
    out_ref = refs[-1]
    owned = out_ref.shape[1]
    for first in range(0, len(refs) - 1, planes):
        mine = refs[first : first + planes]
        rows = mine[0].shape[0]
        devices = slice(first // planes * rows // owned, (first // planes + 1) * rows // owned)
        stats = [m[:, HEAD_COLUMNS : HEAD_COLUMNS + LANES].astype(f32) for m in mine]
        for h in range(PER_KEY):
            logs = [
                s[:, h : h + 1]
                + s[:, PER_KEY + h : PER_KEY + h + 1]
                + s[:, 2 * PER_KEY + h : 2 * PER_KEY + h + 1]
                for s in stats
            ]
            column = slice(h * HEAD_WIDTH, (h + 1) * HEAD_WIDTH)
            merged = merge_head([m[:, column].astype(f32) for m in mine], logs)
            out_ref[devices, :, column] = merged.reshape(-1, owned, HEAD_WIDTH).astype(bf16)


def mix_kernel(query_ref, embed_ref, after_ref, out_ref, sems, *, key_of):
    size = out_ref.shape[0]
    feat = embed_ref.shape[1] // size
    copies = []
    for d in range(size):
        start = key_of[d % GROUP] * HEAD_COLUMNS
        pairs = (
            (query_ref.at[:, start : start + HEAD_COLUMNS], pl.ds(0, HEAD_COLUMNS)),
            (embed_ref.at[:, d * feat : (d + 1) * feat], pl.ds(HEAD_COLUMNS, feat)),
        )
        for i, (source, columns) in enumerate(pairs):
            copies.append(
                pltpu.make_async_copy(source, out_ref.at[d, :, columns], sems.at[2 * d + i])
            )
    for c in copies:
        c.start()
    for c in copies:
        c.wait()


def split_kernel(place_ref, keys_ref, values_ref, tree_keys_ref, tree_values_ref, *refs, seats):
    outs, sems = refs[-len(seats) - 1 : -1], refs[-1]
    positions, owned = keys_ref.shape[0], tree_keys_ref.shape[0]
    copies = []
    for i, r in enumerate(seats):
        seat = place_ref[1] ^ r
        head = (seat >> 1) | ((seat & 1) * (GROUP // 2))
        start = pl.multiple_of(head * HEAD_WIDTH, HEAD_WIDTH)
        for j, (x, y) in enumerate(
            ((keys_ref, tree_keys_ref), (values_ref, tree_values_ref))
        ):
            columns = pl.ds(j * HEAD_WIDTH, HEAD_WIDTH)
            for k, (source, first, rows) in enumerate(((x, 0, positions), (y, positions, owned))):
                copies.append(
                    pltpu.make_async_copy(
                        source.at[:, pl.ds(start, HEAD_WIDTH)],
                        outs[i].at[pl.ds(first, rows), columns],
                        sems.at[4 * i + 2 * j + k],
                    )
                )
    for c in copies:
        c.start()
    for c in copies:
        c.wait()


def join(rows, weight, out_ref, base_ref=None, *, trees, spots):
    _, slots, part = out_ref.shape
    chunks = len(spots) // trees
    for n in range(chunks):
        total = dot(rows, weight[:, n * part : (n + 1) * part])
        for t in range(trees):
            spot = spots[t * chunks + n]
            some = total[t * slots : (t + 1) * slots]
            out_ref[spot] = some if base_ref is None else some + base_ref[spot]


def take_halves(bit, keep_ref, send_ref, *refs):
    half = keep_ref.shape[0]
    for ref, start in ((keep_ref, bit * half), (send_ref, (1 - bit) * half)):
        parts = [r[pl.ds(start, half)] for r in refs]
        ref[...] = functools.reduce(jnp.add, parts)


def halve_kernel(bit_ref, mine_ref, other_ref, keep_ref, send_ref):
    take_halves(bit_ref[0], keep_ref, send_ref, mine_ref, other_ref)


def add_kernel(mine_ref, other_ref, out_ref):
    out_ref[...] = mine_ref[...] + other_ref[...]


def embed_kernel(pick_ref, mix_ref, weight_ref, out_ref, buffer, sems, *, trees, spots):
    depth = weight_ref.shape[0] // WEIGHT_PIECES
    copies = []
    for i in range(WEIGHT_PIECES):
        piece = pl.ds(i * depth, depth)
        copies.append(
            pltpu.make_async_copy(weight_ref.at[piece], buffer.at[piece], sems.at[i])
        )
    for c in copies:
        c.start()
    rows = dot(pick_ref[...], mix_ref[:, HEAD_COLUMNS:]).astype(bf16)
    for c in copies:
        c.wait()
    join(rows, buffer, out_ref, trees=trees, spots=spots)


def feature_kernel(bit_ref, *refs, planes, feat, trees, spots):
    messages = refs[:planes]
    weight_ref, add_ref, keep_ref, send_ref, hold_ref = refs[planes:]
    heads = []
    for h in range(feat // HEAD_WIDTH):
        column = slice(h * HEAD_WIDTH, (h + 1) * HEAD_WIDTH)
        merged = merge_head(
            [m[:, column] for m in messages],
            [m[:, feat + h : feat + h + 1] for m in messages],
        )
        heads.append(merged.astype(bf16))
    rows = heads[0] if len(heads) == 1 else jnp.concatenate(heads, axis=1)
    join(rows, weight_ref, hold_ref, add_ref, trees=trees, spots=spots)
    take_halves(bit_ref[0], keep_ref, send_ref, hold_ref)


def norm_kernel(place_ref, gain_ref, pick_ref, *refs, offsets):
    joined, out_ref = refs[:-1], refs[-1]
    chunks = len(joined)
    _, slots, width = joined[0].shape
    total = jnp.zeros((slots, width), f32)
    for x in joined:
        total = total + x[0] * x[0]
    total = jnp.sum(total, axis=1, keepdims=True)
    factor = lax.rsqrt(total / (chunks * width) + 1e-06)
    pick = pick_ref[...]
    for x, offset in zip(joined, offsets):
        columns = pl.ds(pl.multiple_of((place_ref[0] ^ offset) * width, width), width)
        normed = x[0] * factor * gain_ref[:, columns]
        rows = jnp.zeros((pick.shape[0], width), f32)
        for s in range(slots):
            rows = rows + jnp.where(pick[:, s : s + 1] > 0.5, normed[s : s + 1, :], 0.0)
        out_ref[:, columns] = rows.astype(bf16)


def ancestors(parents):
    nodes = parents.shape[1]
    column = jnp.arange(nodes, dtype=jnp.int32)
    upward = (parents[:, :, None] == column[None, None, :]).astype(f32)
    closure = jnp.maximum(upward, jnp.eye(nodes, dtype=f32)[None])
    for _ in range(3):
        closure = jnp.minimum(jnp.einsum("tij,tjk->tik", closure, closure), 1.0)
    return closure


def body(
    queries,
    prefix_key_heads,
    prefix_value_heads,
    tree_key_heads,
    tree_value_heads,
    token_embed,
    fc_embed,
    fc_feature,
    draft_gain,
    parents,
    accepted,
):
    size = lax.axis_size("ctx")
    me = lax.axis_index("ctx")
    trees, nodes = parents.shape
    owned, model = queries.shape
    positions = prefix_key_heads.shape[0]
    feat = fc_feature.shape[0]
    every_row = trees * nodes
    planes = size // GROUP
    plane, seat = me // GROUP, me % GROUP
    plane_rows = GROUP * owned
    chunks = size // trees
    part = model // chunks
    mixed = HEAD_COLUMNS + feat
    key_of = [(w >> 1) | ((w & 1) * (GROUP // 2)) for w in range(GROUP)]

    scalar = pl.BlockSpec(memory_space=pltpu.SMEM)
    block = pl.BlockSpec(memory_space=pltpu.VMEM)
    outside = pl.BlockSpec(memory_space=pl.ANY)
    stored = pl.BlockSpec(memory_space=pltpu.HBM)
    busy = pl.CostEstimate(flops=4 * 10**9, bytes_accessed=10**6, transcendentals=10**6)
    room = pltpu.CompilerParams(vmem_limit_bytes=ROOM)

    def swap(x, mask):
        return lax.ppermute(x, "ctx", [(s, s ^ mask) for s in range(size)])

    plane_groups = [[p * GROUP + g for g in range(GROUP)] for p in range(planes)]

    def leave(x):
        return pltpu.with_memory_space_constraint(x, pltpu.HBM)

    place = jnp.stack([plane, seat]).astype(jnp.int32)
    sources = [
        leave(x)
        for x in (prefix_key_heads, prefix_value_heads, tree_key_heads, tree_value_heads)
    ]

    def split(seats, after):
        return pl.pallas_call(
            functools.partial(split_kernel, seats=seats),
            in_specs=[scalar] + [stored] * 4 + [outside] * len(after),
            out_specs=[block] * len(seats),
            out_shape=[jax.ShapeDtypeStruct((positions + owned, 2 * HEAD_WIDTH), bf16)]
            * len(seats),
            scratch_shapes=[pltpu.SemaphoreType.DMA((4 * len(seats),))],
            compiler_params=room,
            name="split",
        )(place, *sources, *after)

    slabs = list(split(ARRIVAL[1:5], ()))
    slabs = list(split(ARRIVAL[:1], slabs[:1])) + slabs + list(split(ARRIVAL[5:], slabs[:1]))
    after = slabs[-1]
    for i, r in enumerate(ARRIVAL):
        if r:
            slabs[i] = swap(slabs[i], r)
    tree_kv = jnp.concatenate([s[positions:] for s in slabs], axis=0)
    tree_kv = jnp.pad(tree_kv, ((0, LANES - plane_rows), (0, 0)))
    slabs = [pltpu.with_memory_space_constraint(s, pltpu.VMEM) for s in slabs]

    packed = pl.pallas_call(
        functools.partial(mix_kernel, key_of=key_of),
        in_specs=[stored, stored, outside],
        out_specs=block,
        out_shape=jax.ShapeDtypeStruct((size, owned, mixed), bf16),
        scratch_shapes=[pltpu.SemaphoreType.DMA((2 * size,))],
        compiler_params=room,
        name="pack",
    )(leave(queries), leave(token_embed), after)
    mix = lax.all_to_all(packed, "ctx", split_axis=0, concat_axis=0, tiled=True)
    mix = pltpu.with_memory_space_constraint(mix.reshape(every_row, mixed), pltpu.VMEM)

    closure = ancestors(parents)
    chosen = (accepted[:, None] == jnp.arange(nodes, dtype=jnp.int32)[None, :]).astype(f32)
    on_path = jnp.einsum("ti,tij->tj", chosen, closure)
    upto = (jnp.arange(nodes)[:, None] <= jnp.arange(nodes)[None, :]).astype(f32)
    rank = jnp.dot(on_path, upto)
    slot = jnp.arange(1, SLOTS + 1, dtype=f32)
    pick = jnp.where(
        (rank[:, None, :] == slot[None, :, None]) & (on_path[:, None, :] > 0.5), 1.0, 0.0
    )
    same = jnp.eye(trees, dtype=f32)
    pick_rows = (same[:, None, :, None] * pick[:, :, None, :]).reshape(trees * SLOTS, every_row)
    reach = (same[:, None, :, None] * closure[:, :, None, :]).reshape(every_row, every_row)
    row = jnp.arange(every_row, dtype=jnp.int32)
    key = jnp.arange(LANES, dtype=jnp.int32)
    key_seat = seat ^ jnp.array(ARRIVAL, jnp.int32)[jnp.minimum(key // owned, GROUP - 1)]
    key_row = plane * plane_rows + key_seat * owned + key % owned
    key_row = jnp.where(key < plane_rows, key_row, -1)
    keys_hot = (row[:, None] == key_row[None, :]).astype(f32)
    bias = jnp.where(jnp.dot(reach, keys_hot) > 0.5, 0.0, NEGATIVE)
    pick_rows = pick_rows.astype(bf16)
    bias_picked = jnp.where(jnp.dot(jnp.dot(pick_rows, reach), keys_hot) > 0.5, 0.0, NEGATIVE)
    own_tree = (jnp.arange(trees) == me // chunks).astype(f32)
    own_rows = (me * owned + jnp.arange(owned))[:, None] == row[None, :]
    own_pick = jnp.einsum(
        "rj,tsj->rs",
        own_rows.astype(f32),
        pick_rows.astype(f32).reshape(trees, SLOTS, every_row) * own_tree[:, None, None],
    )

    bits = size.bit_length() - 1
    inner = chunks.bit_length() - 1
    order = [0, *range(inner, bits), *range(1, inner)]
    spots = tuple(
        sum(((d >> bit) & 1) << (bits - 1 - i) for i, bit in enumerate(order))
        for d in range(size)
    )

    def sums(devices):
        return jax.ShapeDtypeStruct((devices, SLOTS, part), f32)

    def bit_of(i):
        return ((me >> order[i]) & 1).astype(jnp.int32)[None]

    embed_part = pl.pallas_call(
        functools.partial(embed_kernel, trees=trees, spots=spots),
        in_specs=[block, block, stored],
        out_specs=block,
        out_shape=sums(size),
        scratch_shapes=[
            pltpu.VMEM((feat, model), bf16),
            pltpu.SemaphoreType.DMA((WEIGHT_PIECES,)),
        ],
        compiler_params=room,
        cost_estimate=busy,
        name="embed_join",
    )(pick_rows, mix, leave(fc_embed))

    messages = pl.pallas_call(
        functools.partial(accepted_kernel, planes=planes, positions=positions, feat=feat),
        in_specs=[scalar] + [block] * (GROUP + 4),
        out_specs=[block] * planes,
        out_shape=[jax.ShapeDtypeStruct((trees * SLOTS, feat + LANES), f32)] * planes,
        scratch_shapes=[pltpu.VMEM((planes, trees * SLOTS, feat + LANES), f32)],
        compiler_params=room,
        cost_estimate=busy,
        name="accepted",
    )(place, mix, *slabs, tree_kv, bias_picked, pick_rows)
    arrived = []
    for k in range(planes):
        target = [
            (p * GROUP + w, planes * key_of[w] + (p ^ k))
            for p in range(planes)
            for w in range(GROUP)
        ]
        arrived.append(lax.ppermute(messages[k], "ctx", target))
    arrived = [pltpu.with_memory_space_constraint(x, pltpu.VMEM) for x in arrived]
    keep, send = pl.pallas_call(
        functools.partial(feature_kernel, planes=planes, feat=feat, trees=trees, spots=spots),
        in_specs=[scalar] + [block] * (planes + 2),
        out_specs=[block] * 2,
        out_shape=[sums(size // 2)] * 2,
        scratch_shapes=[pltpu.VMEM((size, SLOTS, part), f32)],
        compiler_params=room,
        name="feature_join",
    )(bit_of(0), *arrived, fc_feature, embed_part)
    for i, bit in enumerate(order):
        other = swap(send, 1 << bit)
        other = pltpu.with_memory_space_constraint(other, pltpu.VMEM)
        if i + 1 < bits:
            keep, send = pl.pallas_call(
                halve_kernel,
                in_specs=[scalar] + [block] * 2,
                out_specs=[block] * 2,
                out_shape=[sums(size >> (i + 2))] * 2,
                compiler_params=room,
                name="halve",
            )(bit_of(i + 1), keep, other)
        else:
            own = pl.pallas_call(
                add_kernel,
                in_specs=[block] * 2,
                out_specs=block,
                out_shape=sums(1),
                compiler_params=room,
                name="add",
            )(keep, other)
    joined = [own]
    offsets = [0]
    for bit in reversed(range(inner)):
        joined = joined + [swap(x, 1 << bit) for x in joined]
        offsets = offsets + [o ^ (1 << bit) for o in offsets]
    joined = [pltpu.with_memory_space_constraint(x, pltpu.VMEM) for x in joined]
    draft_input = pl.pallas_call(
        functools.partial(norm_kernel, offsets=tuple(offsets)),
        in_specs=[scalar] + [block] * (chunks + 2),
        out_specs=block,
        out_shape=jax.ShapeDtypeStruct((owned, model), bf16),
        compiler_params=room,
        name="norm",
    )((me % chunks).astype(jnp.int32)[None], draft_gain[None, :], own_pick, *joined)

    rows = min(plane_rows, STEP)
    pieces = [(p, f) for p in [*range(1, planes), 0] for f in range(0, plane_rows, rows)]
    gathered = {}
    for p, first in pieces:
        out = pl.pallas_call(
            functools.partial(
                bulk_kernel,
                distance=p,
                first=first,
                plane_rows=plane_rows,
                positions=positions,
            ),
            in_specs=[scalar] + [block] * (GROUP + 3) + [outside],
            out_specs=block,
            out_shape=jax.ShapeDtypeStruct((rows, HEAD_COLUMNS + LANES), bf16),
            compiler_params=room,
            cost_estimate=busy,
        )(place, mix, *slabs, tree_kv, bias, messages[0])
        if p:
            out = swap(out, GROUP * p)
        gathered[first, p] = pltpu.with_memory_space_constraint(out, pltpu.VMEM)
    merged = pl.pallas_call(
        functools.partial(merge_kernel, planes=planes),
        in_specs=[block] * len(pieces),
        out_specs=block,
        out_shape=jax.ShapeDtypeStruct((GROUP, owned, HEAD_COLUMNS), bf16),
        compiler_params=room,
        name="merge",
    )(*[gathered[k] for k in sorted(gathered)])
    by_seat = lax.all_to_all(
        merged,
        "ctx",
        split_axis=0,
        concat_axis=0,
        tiled=True,
        axis_index_groups=plane_groups,
    )
    seat_of = [key_of.index(k) for k in range(GROUP)]
    attended = jnp.concatenate([by_seat[w] for w in seat_of], axis=1)
    return (attended, draft_input)


def solution(mesh):
    placed = (
        P(("groups", "ctx"), None),
        P(("groups", "ctx"), None),
        P(("groups", "ctx"), None),
        P(("groups", "ctx"), None),
        P(("groups", "ctx"), None),
        P(("groups", "ctx"), None),
        P("ctx", None),
        P("ctx", None),
        P(),
        P("groups", None),
        P("groups"),
    )
    return jax.shard_map(
        body,
        mesh=mesh,
        in_specs=placed,
        out_specs=(P(("groups", "ctx"), None), P(("groups", "ctx"), None)),
        check_vma=False,
    )
```

profile of v0, /device:TPU:0, one launch (start us, length us, event | category | flops | bytes accessed | tf_op | source)
XLA Modules:
  0.0 108.4 jit_solution(3774099707092795391)
XLA Ops:
  0.7 2.9 %split.3 = (bf16[520,256]{1,0:T(8,128)(2,1)S(1)}, bf16[520,256]{1,0:T(8,128)(2,1)S(1)}, bf16[520,256]{1,0:T(8,128)(2,1)}, bf16[520,256]{1,0:T(8,128)(2,1)}) custom-call(s32[2]{0:T(128)S(1)} %pad_add_fusion.place_ref, bf16[512,1024]{1,0:T(8,128)(2,1)} %keys_ref.5, bf16[512,1024]{1,0:T(8,128)(2,1)} %values_ref.5, bf16[8,1024]{1,0:T(8,128)(2,1)} %tree_keys_ref.5, ...), custom_call_target="tpu_custom_call" | custom-call | tf_op jit(solution)/shard_map/split/pallas_call | solution.py:320
  3.6 3.1 %collective-permute-start = (bf16[520,256]{1,0:T(8,128)(2,1)S(1)}, bf16[520,256]{1,0:T(8,128)(2,1)S(1)}, u32[]{:S(2)}, u32[]{:S(2)}) collective-permute-start(bf16[520,256]{1,0:T(8,128)(2,1)S(1)} %get-tuple-element.19.refs_0_), channel_id=1, source_target_pairs={{0,2},{1,3},{2,0},{3,1},{4,6},{5,7},{6,4},{7,5},{8,10},{9,11},{10,... | collective-permute-start | bytes 798728 | tf_op jit(solution)/shard_map/ppermute | solution.py:306
  6.7 2.7 %split.4 = (bf16[520,256]{1,0:T(8,128)(2,1)}, bf16[520,256]{1,0:T(8,128)(2,1)S(1)}, bf16[520,256]{1,0:T(8,128)(2,1)S(1)}) custom-call(s32[2]{0:T(128)S(1)} %pad_add_fusion.place_ref, bf16[512,1024]{1,0:T(8,128)(2,1)} %keys_ref.5, bf16[512,1024]{1,0:T(8,128)(2,1)} %values_ref.5, bf16[8,1024]{1,0:T(8,128)(2,1)} %tree_keys_ref.5, ...), custom_call_target="tpu_custom_call" | custom-call | tf_op jit(solution)/shard_map/split/pallas_call | solution.py:320
  9.4 2.0 %pack.1 = bf16[16,8,1536]{2,1,0:T(8,128)(2,1)} custom-call(bf16[8,8192]{1,0:T(8,128)(2,1)} %query_ref.1, bf16[8,8192]{1,0:T(8,128)(2,1)} %embed_ref.1, bf16[520,256]{1,0:T(8,128)(2,1)S(1)} %get-tuple-element.20.after_ref), custom_call_target="tpu_custom_call" | custom-call | tf_op jit(solution)/shard_map/pack/pallas_call | solution.py:341
  11.4 5.1 %all-to-all-start = ((bf16[16,8,1536]{2,1,0:T(8,128)(2,1)}), bf16[16,8,1536]{2,1,0:T(8,128)(2,1)S(1)}, u32[]{:S(2)}, u32[]{:S(2)}) async-start(bf16[16,8,1536]{2,1,0:T(8,128)(2,1)} %pack.1), calls=%async_computation | async-start | bytes 786432 | tf_op jit(solution)/shard_map/all_to_all | solution.py:350
  16.5 1.9 %collective-permute-start.1 = (bf16[520,256]{1,0:T(8,128)(2,1)S(1)}, bf16[520,256]{1,0:T(8,128)(2,1)S(1)}, u32[]{:S(2)}, u32[]{:S(2)}) collective-permute-start(bf16[520,256]{1,0:T(8,128)(2,1)S(1)} %get-tuple-element.21), channel_id=1, source_target_pairs={{0,4},{1,5},{2,6},{3,7},{4,0},{5,1},{6,2},{7,3},{8,12},{9,13},{10,... | collective-permute-start | bytes 798728 | tf_op jit(solution)/shard_map/ppermute | solution.py:306
  18.4 0.9 collective-permute-start.2
  19.4 0.8 collective-permute-start.3
  20.2 1.0 convolution_minimum_fusion.2
  21.2 0.3 convolution_minimum_fusion
  21.5 0.7 compare_bitcast_fusion
  22.2 0.1 fusion.20
  22.3 0.1 fusion.18
  23.0 0.1 fusion.refs_9_
  23.1 0.2 fusion.7.refs_9_
  23.4 1.6 %split.5.refs_0_ = bf16[520,256]{1,0:T(8,128)(2,1)S(1)} custom-call(s32[2]{0:T(128)S(1)} %pad_add_fusion.place_ref, bf16[512,1024]{1,0:T(8,128)(2,1)} %keys_ref.5, bf16[512,1024]{1,0:T(8,128)(2,1)} %values_ref.5, bf16[8,1024]{1,0:T(8,128)(2,1)} %tree_keys_ref.5, bf16[8,1024]{1,0:T(8,128)(2,1)} %tree_values_ref.5, bf16[520,256]{1,0:T(8,128)(2,1)S(1)} %get-tuple-element.19.refs_0_), custom_call_target="tpu_custom_call" | custom-call | tf_op jit(solution)/shard_map/split/pallas_call | solution.py:320
  25.0 1.5 %collective-permute-start.4 = (bf16[520,256]{1,0:T(8,128)(2,1)}, bf16[520,256]{1,0:T(8,128)(2,1)S(1)}, u32[]{:S(2)}, u32[]{:S(2)}) collective-permute-start(bf16[520,256]{1,0:T(8,128)(2,1)} %get-tuple-element.24), channel_id=1, source_target_pairs={{0,6},{1,7},{2,4},{3,5},{4,2},{5,3},{6,0},{7,1},{8,14},{9,15},{10,... | collective-permute-start | bytes 798728 | tf_op jit(solution)/shard_map/ppermute | solution.py:306
  26.5 5.7 %collective-permute-done.1.refs_2_ = bf16[520,256]{1,0:T(8,128)(2,1)S(1)} collective-permute-done((bf16[520,256]{1,0:T(8,128)(2,1)S(1)}, bf16[520,256]{1,0:T(8,128)(2,1)S(1)}, u32[]{:S(2)}, u32[]{:S(2)}) %collective-permute-start.1) | collective-permute-done | bytes 266272 | tf_op jit(solution)/shard_map/ppermute | solution.py:306
  32.3 4.5 %collective-permute-done.3.refs_4_ = bf16[520,256]{1,0:T(8,128)(2,1)S(1)} collective-permute-done((bf16[520,256]{1,0:T(8,128)(2,1)}, bf16[520,256]{1,0:T(8,128)(2,1)S(1)}, u32[]{:S(2)}, u32[]{:S(2)}) %collective-permute-start.3) | collective-permute-done | bytes 266272 | tf_op jit(solution)/shard_map/ppermute | solution.py:306
  36.8 7.7 %collective-permute-done.4.refs_5_ = bf16[520,256]{1,0:T(8,128)(2,1)S(1)} collective-permute-done((bf16[520,256]{1,0:T(8,128)(2,1)}, bf16[520,256]{1,0:T(8,128)(2,1)S(1)}, u32[]{:S(2)}, u32[]{:S(2)}) %collective-permute-start.4) | collective-permute-done | bytes 266272 | tf_op jit(solution)/shard_map/ppermute | solution.py:306
  44.5 4.6 %collective-permute-done.5.refs_6_ = bf16[520,256]{1,0:T(8,128)(2,1)S(1)} collective-permute-done((bf16[520,256]{1,0:T(8,128)(2,1)S(1)}, bf16[520,256]{1,0:T(8,128)(2,1)S(1)}, u32[]{:S(2)}, u32[]{:S(2)}) %collective-permute-start.5) | collective-permute-done | bytes 266272 | tf_op jit(solution)/shard_map/ppermute | solution.py:306
  49.1 2.0 %accepted.1 = (f32[16,640]{1,0:T(8,128)S(1)}, f32[16,640]{1,0:T(8,128)S(1)}) custom-call(s32[2]{0:T(128)S(1)} %pad_add_fusion.place_ref, bf16[128,1536]{1,0:T(8,128)(2,1)S(1)} %bitcast.76, bf16[520,256]{1,0:T(8,128)(2,1)S(1)} %split.5.refs_0_, bf16[520,256]{1,0:T(8,128)(2,1)S(1)} %collective-permute-done.refs_1_, ...), custom_call_target="tpu_custom_call" | custom-call | flops 4000000000 | bytes 1000000 | tf_op jit(solution)/shard_map/accepted/pallas_call | solution.py:410
  51.1 0.7 collective-permute-start.9
  51.8 2.7 %shard_map.132 = bf16[32,1152]{1,0:T(8,128)(2,1)S(1)} custom-call(s32[2]{0:T(128)S(1)} %pad_add_fusion.place_ref, bf16[128,1536]{1,0:T(8,128)(2,1)S(1)} %bitcast.77, bf16[520,256]{1,0:T(8,128)(2,1)S(1)} %split.5.refs_0_, bf16[520,256]{1,0:T(8,128)(2,1)S(1)} %collective-permute-done.refs_1_, bf16[520,256]{1,0:T(8,128)(2,1)S(1)} %collective-permute-done.1.refs_2_, ...), custom_call_target="tpu_custom_call" | custom-call | flops 4000000000 | bytes 1000000 | tf_op jit(solution)/shard_map/pallas_call | solution.py:478
  54.5 4.2 %collective-permute-start.7 = (bf16[32,1152]{1,0:T(8,128)(2,1)S(1)}, bf16[32,1152]{1,0:T(8,128)(2,1)S(1)}, u32[]{:S(2)}, u32[]{:S(2)}) collective-permute-start(bf16[32,1152]{1,0:T(8,128)(2,1)S(1)} %shard_map.132), channel_id=1, source_target_pairs={{0,8},{1,9},{2,10},{3,11},{4,12},{5,13},{6,14},{7,15},{8,0},{9,1},... | collective-permute-start | bytes 221192 | tf_op jit(solution)/shard_map/ppermute | solution.py:306
  58.7 2.7 %shard_map.134 = bf16[32,1152]{1,0:T(8,128)(2,1)S(1)} custom-call(s32[2]{0:T(128)S(1)} %pad_add_fusion.place_ref, bf16[128,1536]{1,0:T(8,128)(2,1)S(1)} %bitcast.78, bf16[520,256]{1,0:T(8,128)(2,1)S(1)} %split.5.refs_0_, bf16[520,256]{1,0:T(8,128)(2,1)S(1)} %collective-permute-done.refs_1_, bf16[520,256]{1,0:T(8,128)(2,1)S(1)} %collective-permute-done.1.refs_2_, ...), custom_call_target="tpu_custom_call" | custom-call | flops 4000000000 | bytes 1000000 | tf_op jit(solution)/shard_map/pallas_call | solution.py:478
  61.5 1.9 %collective-permute-start.10 = (f32[16,640]{1,0:T(8,128)S(1)}, f32[16,640]{1,0:T(8,128)S(1)}, u32[]{:S(2)}, u32[]{:S(2)}) collective-permute-start(f32[16,640]{1,0:T(8,128)S(1)} %get-tuple-element.27), channel_id=1, source_target_pairs={{0,1},{1,9},{2,3},{3,11},{4,5},{5,13},{6,7},{7,15},{8,0},{9,8},{10... | collective-permute-start | bytes 122888 | tf_op jit(solution)/shard_map/ppermute | solution.py:427
  63.5 4.7 %embed_join.1.refs_3_ = f32[16,8,1024]{2,1,0:T(8,128)S(1)} custom-call(bf16[16,128]{1,0:T(8,128)(2,1)S(1)} %convert_element_type.46.refs_10_.pick_ref, bf16[128,1536]{1,0:T(8,128)(2,1)S(1)} %bitcast.79, bf16[512,8192]{1,0:T(8,128)(2,1)} %weight_ref.1), custom_call_target="tpu_custom_call" | custom-call | flops 4000000000 | bytes 1000000 | tf_op jit(solution)/shard_map/embed_join/pallas_call | solution.py:396
  68.2 2.7 %shard_map.131.refs_0_ = bf16[32,1152]{1,0:T(8,128)(2,1)S(1)} custom-call(s32[2]{0:T(128)S(1)} %pad_add_fusion.place_ref, bf16[128,1536]{1,0:T(8,128)(2,1)S(1)} %bitcast.80, bf16[520,256]{1,0:T(8,128)(2,1)S(1)} %split.5.refs_0_, bf16[520,256]{1,0:T(8,128)(2,1)S(1)} %collective-permute-done.refs_1_, bf16[520,256]{1,0:T(8,128)(2,1)S(1)} %collective-permute-done.1.refs_2_, ...), custom_call_target="tpu_custom_call" | custom-call | flops 4000000000 | bytes 1000000 | tf_op jit(solution)/shard_map/pallas_call | solution.py:478
  70.9 2.7 %shard_map.133.refs_2_ = bf16[32,1152]{1,0:T(8,128)(2,1)S(1)} custom-call(s32[2]{0:T(128)S(1)} %pad_add_fusion.place_ref, bf16[128,1536]{1,0:T(8,128)(2,1)S(1)} %bitcast.81, bf16[520,256]{1,0:T(8,128)(2,1)S(1)} %split.5.refs_0_, bf16[520,256]{1,0:T(8,128)(2,1)S(1)} %collective-permute-done.refs_1_, bf16[520,256]{1,0:T(8,128)(2,1)S(1)} %collective-permute-done.1.refs_2_, ...), custom_call_target="tpu_custom_call" | custom-call | flops 4000000000 | bytes 1000000 | tf_op jit(solution)/shard_map/pallas_call | solution.py:478
  73.7 1.3 %feature_join.1 = (f32[8,8,1024]{2,1,0:T(8,128)S(1)}, f32[8,8,1024]{2,1,0:T(8,128)S(1)}) custom-call(s32[1]{0:T(128)} %bitcast.20.bit_ref, f32[16,640]{1,0:T(8,128)S(1)} %collective-permute-done.9.refs_0_, f32[16,640]{1,0:T(8,128)S(1)} %collective-permute-done.10.refs_1_, bf16[512,8192]{1,0:T(8,128)(2,1)S(1)} %bitcast.75, f32[16,8,1024]{2,1,0:T(8,128)S(1)} %embed_join.1.refs_3_), custom_call_target="tpu_custom_call" | custom-call | tf_op jit(solution)/shard_map/feature_join/pallas_call | solution.py:429
  75.0 0.3 collective-permute-start.11
  75.4 1.2 %merge.1 = bf16[8,8,1024]{2,1,0:T(8,128)(2,1)} custom-call(bf16[32,1152]{1,0:T(8,128)(2,1)S(1)} %shard_map.131.refs_0_, bf16[32,1152]{1,0:T(8,128)(2,1)S(1)} %collective-permute-done.7.refs_1_, bf16[32,1152]{1,0:T(8,128)(2,1)S(1)} %shard_map.133.refs_2_, bf16[32,1152]{1,0:T(8,128)(2,1)S(1)} %collective-permute-done.8.refs_3_), custom_call_target="tpu_custom_call" | custom-call | tf_op jit(solution)/shard_map/merge/pallas_call | solution.py:495
  76.5 3.4 %all-to-all-start.1 = ((bf16[8,8,1024]{2,1,0:T(8,128)(2,1)}), bf16[8,8,1024]{2,1,0:T(8,128)(2,1)S(1)}, u32[]{:S(2)}, u32[]{:S(2)}) async-start(bf16[8,8,1024]{2,1,0:T(8,128)(2,1)} %merge.1), calls=%async_computation.1 | async-start | bytes 262144 | tf_op jit(solution)/shard_map/all_to_all | solution.py:503
  80.0 0.2 fusion.19.pick_ref
  80.2 1.3 %collective-permute-start.12 = (f32[4,8,1024]{2,1,0:T(8,128)S(1)}, f32[4,8,1024]{2,1,0:T(8,128)S(1)}, u32[]{:S(2)}, u32[]{:S(2)}) collective-permute-start(f32[4,8,1024]{2,1,0:T(8,128)S(1)} %get-tuple-element.31), channel_id=1, source_target_pairs={{0,8},{1,9},{2,10},{3,11},{4,12},{5,13},{6,14},{7,15},{8,0},{9,1},... | collective-permute-start | bytes 393224 | tf_op jit(solution)/shard_map/ppermute | solution.py:306
  81.5 4.1 %all-to-all-done.1 = bf16[8,8,1024]{2,1,0:T(8,128)(2,1)S(1)} async-done(((bf16[8,8,1024]{2,1,0:T(8,128)(2,1)}), bf16[8,8,1024]{2,1,0:T(8,128)(2,1)S(1)}, u32[]{:S(2)}, u32[]{:S(2)}) %all-to-all-start.1) | async-done | bytes 131104 | tf_op jit(solution)/shard_map/all_to_all | solution.py:503
  85.6 4.3 %collective-permute-done.12.other_ref = f32[4,8,1024]{2,1,0:T(8,128)S(1)} collective-permute-done((f32[4,8,1024]{2,1,0:T(8,128)S(1)}, f32[4,8,1024]{2,1,0:T(8,128)S(1)}, u32[]{:S(2)}, u32[]{:S(2)}) %collective-permute-start.12) | collective-permute-done | bytes 131104 | tf_op jit(solution)/shard_map/ppermute | solution.py:306
  89.9 1.7 %collective-permute-start.13 = (f32[2,8,1024]{2,1,0:T(8,128)S(1)}, f32[2,8,1024]{2,1,0:T(8,128)S(1)}, u32[]{:S(2)}, u32[]{:S(2)}) collective-permute-start(f32[2,8,1024]{2,1,0:T(8,128)S(1)} %get-tuple-element.33), channel_id=1, source_target_pairs={{0,2},{1,3},{2,0},{3,1},{4,6},{5,7},{6,4},{7,5},{8,10},{9,11},{10,... | collective-permute-start | bytes 196616 | tf_op jit(solution)/shard_map/ppermute | solution.py:306
  91.5 2.7 %collective-permute-done.13.other_ref = f32[2,8,1024]{2,1,0:T(8,128)S(1)} collective-permute-done((f32[2,8,1024]{2,1,0:T(8,128)S(1)}, f32[2,8,1024]{2,1,0:T(8,128)S(1)}, u32[]{:S(2)}, u32[]{:S(2)}) %collective-permute-start.13) | collective-permute-done | bytes 65568 | tf_op jit(solution)/shard_map/ppermute | solution.py:306
  94.3 4.1 %collective-permute-done.14.other_ref = f32[1,8,1024]{2,1,0:T(8,128)S(1)} collective-permute-done((f32[1,8,1024]{2,1,0:T(8,128)S(1)}, f32[1,8,1024]{2,1,0:T(8,128)S(1)}, u32[]{:S(2)}, u32[]{:S(2)}) %collective-permute-start.14) | collective-permute-done | bytes 32800 | tf_op jit(solution)/shard_map/ppermute | solution.py:306
  98.4 1.8 %collective-permute-start.16 = (f32[1,8,1024]{2,1,0:T(8,128)S(1)}, f32[1,8,1024]{2,1,0:T(8,128)S(1)}, u32[]{:S(2)}, u32[]{:S(2)}) collective-permute-start(f32[1,8,1024]{2,1,0:T(8,128)S(1)} %add.108.refs_0_), channel_id=1, source_target_pairs={{0,2},{1,3},{2,0},{3,1},{4,6},{5,7},{6,4},{7,5},{8,10},{9,11},{10,... | collective-permute-start | bytes 98312 | tf_op jit(solution)/shard_map/ppermute | solution.py:306
  100.2 2.1 %collective-permute-done.15.refs_1_ = f32[1,8,1024]{2,1,0:T(8,128)S(1)} collective-permute-done((f32[1,8,1024]{2,1,0:T(8,128)S(1)}, f32[1,8,1024]{2,1,0:T(8,128)S(1)}, u32[]{:S(2)}, u32[]{:S(2)}) %collective-permute-start.15) | collective-permute-done | bytes 32800 | tf_op jit(solution)/shard_map/ppermute | solution.py:306
  102.3 1.7 %collective-permute-start.17 = (f32[1,8,1024]{2,1,0:T(8,128)S(1)}, f32[1,8,1024]{2,1,0:T(8,128)S(1)}, u32[]{:S(2)}, u32[]{:S(2)}) collective-permute-start(f32[1,8,1024]{2,1,0:T(8,128)S(1)} %collective-permute-done.15.refs_1_), channel_id=1, source_target_pairs={{0,2},{1,3},{2,0},{3,1},{4,6},{5,7},{6,4},{7,5},{8,10},{9,11},{10,... | collective-permute-start | bytes 98312 | tf_op jit(solution)/shard_map/ppermute | solution.py:306
  104.0 0.5 collective-permute-start.19
  104.5 1.7 %collective-permute-done.17.refs_3_ = f32[1,8,1024]{2,1,0:T(8,128)S(1)} collective-permute-done((f32[1,8,1024]{2,1,0:T(8,128)S(1)}, f32[1,8,1024]{2,1,0:T(8,128)S(1)}, u32[]{:S(2)}, u32[]{:S(2)}) %collective-permute-start.17) | collective-permute-done | bytes 32800 | tf_op jit(solution)/shard_map/ppermute | solution.py:306
  106.2 1.2 %collective-permute-done.21.refs_7_ = f32[1,8,1024]{2,1,0:T(8,128)S(1)} collective-permute-done((f32[1,8,1024]{2,1,0:T(8,128)S(1)}, f32[1,8,1024]{2,1,0:T(8,128)S(1)}, u32[]{:S(2)}, u32[]{:S(2)}) %collective-permute-start.21) | collective-permute-done | bytes 32800 | tf_op jit(solution)/shard_map/ppermute | solution.py:306
  107.4 1.0 norm.1
  (65 shorter events, 1.1 us)
Async XLA Ops:
  3.6 21.4 %collective-permute-start = (bf16[520,256]{1,0:T(8,128)(2,1)S(1)}, bf16[520,256]{1,0:T(8,128)(2,1)S(1)}, u32[]{:S(2)}, u32[]{:S(2)}) collective-permute-start(bf16[520,256]{1,0:T(8,128)(2,1)S(1)} %get-tuple-element.19.refs_0_), channel_id=1, source_target_pairs={{0,2},{1,3},{2,0},{3,1},{4,6},{5,7},{6,4},{7,5},{8,10},{9,11},{10,... | collective-permute-start | bytes 798728 | tf_op jit(solution)/shard_map/ppermute | solution.py:306
  9.3 39.8 %collective-permute-start.6 = (bf16[520,256]{1,0:T(8,128)(2,1)S(1)}, bf16[520,256]{1,0:T(8,128)(2,1)S(1)}, u32[]{:S(2)}, u32[]{:S(2)}) collective-permute-start(bf16[520,256]{1,0:T(8,128)(2,1)S(1)} %get-tuple-element.20.after_ref), channel_id=1, source_target_pairs={{0,1},{1,0},{2,3},{3,2},{4,5},{5,4},{6,7},{7,6},{8,9},{9,8},{10,11... | collective-permute-start | bytes 798728 | tf_op jit(solution)/shard_map/ppermute | solution.py:306
  11.4 37.7 %all-to-all-start = ((bf16[16,8,1536]{2,1,0:T(8,128)(2,1)}), bf16[16,8,1536]{2,1,0:T(8,128)(2,1)S(1)}, u32[]{:S(2)}, u32[]{:S(2)}) async-start(bf16[16,8,1536]{2,1,0:T(8,128)(2,1)} %pack.1), calls=%async_computation | async-start | bytes 786432 | tf_op jit(solution)/shard_map/all_to_all | solution.py:350
  16.5 15.7 %collective-permute-start.1 = (bf16[520,256]{1,0:T(8,128)(2,1)S(1)}, bf16[520,256]{1,0:T(8,128)(2,1)S(1)}, u32[]{:S(2)}, u32[]{:S(2)}) collective-permute-start(bf16[520,256]{1,0:T(8,128)(2,1)S(1)} %get-tuple-element.21), channel_id=1, source_target_pairs={{0,4},{1,5},{2,6},{3,7},{4,0},{5,1},{6,2},{7,3},{8,12},{9,13},{10,... | collective-permute-start | bytes 798728 | tf_op jit(solution)/shard_map/ppermute | solution.py:306
  18.4 13.8 %collective-permute-start.2 = (bf16[520,256]{1,0:T(8,128)(2,1)}, bf16[520,256]{1,0:T(8,128)(2,1)S(1)}, u32[]{:S(2)}, u32[]{:S(2)}) collective-permute-start(bf16[520,256]{1,0:T(8,128)(2,1)} %get-tuple-element.22), channel_id=1, source_target_pairs={{0,3},{1,2},{2,1},{3,0},{4,7},{5,6},{6,5},{7,4},{8,11},{9,10},{10,... | collective-permute-start | bytes 798728 | tf_op jit(solution)/shard_map/ppermute | solution.py:306
  19.4 17.4 %collective-permute-start.3 = (bf16[520,256]{1,0:T(8,128)(2,1)}, bf16[520,256]{1,0:T(8,128)(2,1)S(1)}, u32[]{:S(2)}, u32[]{:S(2)}) collective-permute-start(bf16[520,256]{1,0:T(8,128)(2,1)} %get-tuple-element.23), channel_id=1, source_target_pairs={{0,5},{1,4},{2,7},{3,6},{4,1},{5,0},{6,3},{7,2},{8,13},{9,12},{10,... | collective-permute-start | bytes 798728 | tf_op jit(solution)/shard_map/ppermute | solution.py:306
  25.0 19.6 %collective-permute-start.4 = (bf16[520,256]{1,0:T(8,128)(2,1)}, bf16[520,256]{1,0:T(8,128)(2,1)S(1)}, u32[]{:S(2)}, u32[]{:S(2)}) collective-permute-start(bf16[520,256]{1,0:T(8,128)(2,1)} %get-tuple-element.24), channel_id=1, source_target_pairs={{0,6},{1,7},{2,4},{3,5},{4,2},{5,3},{6,0},{7,1},{8,14},{9,15},{10,... | collective-permute-start | bytes 798728 | tf_op jit(solution)/shard_map/ppermute | solution.py:306
  32.2 16.9 %collective-permute-start.5 = (bf16[520,256]{1,0:T(8,128)(2,1)S(1)}, bf16[520,256]{1,0:T(8,128)(2,1)S(1)}, u32[]{:S(2)}, u32[]{:S(2)}) collective-permute-start(bf16[520,256]{1,0:T(8,128)(2,1)S(1)} %get-tuple-element.25), channel_id=1, source_target_pairs={{0,7},{1,6},{2,5},{3,4},{4,3},{5,2},{6,1},{7,0},{8,15},{9,14},{10,... | collective-permute-start | bytes 798728 | tf_op jit(solution)/shard_map/ppermute | solution.py:306
  51.1 22.6 %collective-permute-start.9 = (f32[16,640]{1,0:T(8,128)S(1)}, f32[16,640]{1,0:T(8,128)S(1)}, u32[]{:S(2)}, u32[]{:S(2)}) collective-permute-start(f32[16,640]{1,0:T(8,128)S(1)} %get-tuple-element.26.refs_10_), channel_id=1, source_target_pairs={{0,0},{1,8},{2,2},{3,10},{4,4},{5,12},{6,6},{7,14},{8,1},{9,9},{10... | collective-permute-start | bytes 122888 | tf_op jit(solution)/shard_map/ppermute | solution.py:427
  54.5 20.9 %collective-permute-start.7 = (bf16[32,1152]{1,0:T(8,128)(2,1)S(1)}, bf16[32,1152]{1,0:T(8,128)(2,1)S(1)}, u32[]{:S(2)}, u32[]{:S(2)}) collective-permute-start(bf16[32,1152]{1,0:T(8,128)(2,1)S(1)} %shard_map.132), channel_id=1, source_target_pairs={{0,8},{1,9},{2,10},{3,11},{4,12},{5,13},{6,14},{7,15},{8,0},{9,1},... | collective-permute-start | bytes 221192 | tf_op jit(solution)/shard_map/ppermute | solution.py:306
  61.5 13.9 %collective-permute-start.8 = (bf16[32,1152]{1,0:T(8,128)(2,1)S(1)}, bf16[32,1152]{1,0:T(8,128)(2,1)S(1)}, u32[]{:S(2)}, u32[]{:S(2)}) collective-permute-start(bf16[32,1152]{1,0:T(8,128)(2,1)S(1)} %shard_map.134), channel_id=1, source_target_pairs={{0,8},{1,9},{2,10},{3,11},{4,12},{5,13},{6,14},{7,15},{8,0},{9,1},... | collective-permute-start | bytes 221192 | tf_op jit(solution)/shard_map/ppermute | solution.py:306
  61.5 12.1 %collective-permute-start.10 = (f32[16,640]{1,0:T(8,128)S(1)}, f32[16,640]{1,0:T(8,128)S(1)}, u32[]{:S(2)}, u32[]{:S(2)}) collective-permute-start(f32[16,640]{1,0:T(8,128)S(1)} %get-tuple-element.27), channel_id=1, source_target_pairs={{0,1},{1,9},{2,3},{3,11},{4,5},{5,13},{6,7},{7,15},{8,0},{9,8},{10... | collective-permute-start | bytes 122888 | tf_op jit(solution)/shard_map/ppermute | solution.py:427
  68.2 5.5 %slice-start = ((s8[8388608]{0:T(1024)(128)(4,1)}), s8[4194304]{0:T(1024)(128)(4,1)S(1)}, s32[]{:S(2)}) async-start(s8[8388608]{0:T(1024)(128)(4,1)} %bitcast.74), calls=%async_computation.2 | async-start | bytes 8388608
  70.9 2.8 %slice-start.1 = ((s8[8388608]{0:T(1024)(128)(4,1)}), s8[4194304]{0:T(1024)(128)(4,1)S(1)}, s32[]{:S(2)}) async-start(s8[8388608]{0:T(1024)(128)(4,1)} %bitcast.74), calls=%async_computation.3 | async-start | bytes 8388608
  73.7 33.8 %copy-start = (f32[8192]{0:T(1024)S(1)}, f32[8192]{0:T(1024)}, u32[]{:S(2)}) copy-start(f32[8192]{0:T(1024)} %param.20) | copy-start | bytes 98308
  75.0 5.2 %collective-permute-start.11 = (f32[8,8,1024]{2,1,0:T(8,128)S(1)}, f32[8,8,1024]{2,1,0:T(8,128)S(1)}, u32[]{:S(2)}, u32[]{:S(2)}) collective-permute-start(f32[8,8,1024]{2,1,0:T(8,128)S(1)} %get-tuple-element.29), channel_id=1, source_target_pairs={{0,1},{1,0},{2,3},{3,2},{4,5},{5,4},{6,7},{7,6},{8,9},{9,8},{10,11... | collective-permute-start | bytes 786440 | tf_op jit(solution)/shard_map/ppermute | solution.py:306
  76.5 9.1 %all-to-all-start.1 = ((bf16[8,8,1024]{2,1,0:T(8,128)(2,1)}), bf16[8,8,1024]{2,1,0:T(8,128)(2,1)S(1)}, u32[]{:S(2)}, u32[]{:S(2)}) async-start(bf16[8,8,1024]{2,1,0:T(8,128)(2,1)} %merge.1), calls=%async_computation.1 | async-start | bytes 262144 | tf_op jit(solution)/shard_map/all_to_all | solution.py:503
  80.2 9.6 %collective-permute-start.12 = (f32[4,8,1024]{2,1,0:T(8,128)S(1)}, f32[4,8,1024]{2,1,0:T(8,128)S(1)}, u32[]{:S(2)}, u32[]{:S(2)}) collective-permute-start(f32[4,8,1024]{2,1,0:T(8,128)S(1)} %get-tuple-element.31), channel_id=1, source_target_pairs={{0,8},{1,9},{2,10},{3,11},{4,12},{5,13},{6,14},{7,15},{8,0},{9,1},... | collective-permute-start | bytes 393224 | tf_op jit(solution)/shard_map/ppermute | solution.py:306
  89.9 4.3 %collective-permute-start.13 = (f32[2,8,1024]{2,1,0:T(8,128)S(1)}, f32[2,8,1024]{2,1,0:T(8,128)S(1)}, u32[]{:S(2)}, u32[]{:S(2)}) collective-permute-start(f32[2,8,1024]{2,1,0:T(8,128)S(1)} %get-tuple-element.33), channel_id=1, source_target_pairs={{0,2},{1,3},{2,0},{3,1},{4,6},{5,7},{6,4},{7,5},{8,10},{9,11},{10,... | collective-permute-start | bytes 196616 | tf_op jit(solution)/shard_map/ppermute | solution.py:306
  94.2 4.1 %collective-permute-start.14 = (f32[1,8,1024]{2,1,0:T(8,128)S(1)}, f32[1,8,1024]{2,1,0:T(8,128)S(1)}, u32[]{:S(2)}, u32[]{:S(2)}) collective-permute-start(f32[1,8,1024]{2,1,0:T(8,128)S(1)} %get-tuple-element.35), channel_id=1, source_target_pairs={{0,4},{1,5},{2,6},{3,7},{4,0},{5,1},{6,2},{7,3},{8,12},{9,13},{10,... | collective-permute-start | bytes 98312 | tf_op jit(solution)/shard_map/ppermute | solution.py:306
  98.4 3.9 %collective-permute-start.15 = (f32[1,8,1024]{2,1,0:T(8,128)S(1)}, f32[1,8,1024]{2,1,0:T(8,128)S(1)}, u32[]{:S(2)}, u32[]{:S(2)}) collective-permute-start(f32[1,8,1024]{2,1,0:T(8,128)S(1)} %add.108.refs_0_), channel_id=1, source_target_pairs={{0,4},{1,5},{2,6},{3,7},{4,0},{5,1},{6,2},{7,3},{8,12},{9,13},{10,... | collective-permute-start | bytes 98312 | tf_op jit(solution)/shard_map/ppermute | solution.py:306
  98.4 6.1 %collective-permute-start.16 = (f32[1,8,1024]{2,1,0:T(8,128)S(1)}, f32[1,8,1024]{2,1,0:T(8,128)S(1)}, u32[]{:S(2)}, u32[]{:S(2)}) collective-permute-start(f32[1,8,1024]{2,1,0:T(8,128)S(1)} %add.108.refs_0_), channel_id=1, source_target_pairs={{0,2},{1,3},{2,0},{3,1},{4,6},{5,7},{6,4},{7,5},{8,10},{9,11},{10,... | collective-permute-start | bytes 98312 | tf_op jit(solution)/shard_map/ppermute | solution.py:306
  102.3 3.9 %collective-permute-start.17 = (f32[1,8,1024]{2,1,0:T(8,128)S(1)}, f32[1,8,1024]{2,1,0:T(8,128)S(1)}, u32[]{:S(2)}, u32[]{:S(2)}) collective-permute-start(f32[1,8,1024]{2,1,0:T(8,128)S(1)} %collective-permute-done.15.refs_1_), channel_id=1, source_target_pairs={{0,2},{1,3},{2,0},{3,1},{4,6},{5,7},{6,4},{7,5},{8,10},{9,11},{10,... | collective-permute-start | bytes 98312 | tf_op jit(solution)/shard_map/ppermute | solution.py:306
  104.0 2.2 %collective-permute-start.18 = (f32[1,8,1024]{2,1,0:T(8,128)S(1)}, f32[1,8,1024]{2,1,0:T(8,128)S(1)}, u32[]{:S(2)}, u32[]{:S(2)}) collective-permute-start(f32[1,8,1024]{2,1,0:T(8,128)S(1)} %add.108.refs_0_), channel_id=1, source_target_pairs={{0,1},{1,0},{2,3},{3,2},{4,5},{5,4},{6,7},{7,6},{8,9},{9,8},{10,11... | collective-permute-start | bytes 98312 | tf_op jit(solution)/shard_map/ppermute | solution.py:306
  104.0 2.2 %collective-permute-start.19 = (f32[1,8,1024]{2,1,0:T(8,128)S(1)}, f32[1,8,1024]{2,1,0:T(8,128)S(1)}, u32[]{:S(2)}, u32[]{:S(2)}) collective-permute-start(f32[1,8,1024]{2,1,0:T(8,128)S(1)} %collective-permute-done.15.refs_1_), channel_id=1, source_target_pairs={{0,1},{1,0},{2,3},{3,2},{4,5},{5,4},{6,7},{7,6},{8,9},{9,8},{10,11... | collective-permute-start | bytes 98312 | tf_op jit(solution)/shard_map/ppermute | solution.py:306
  104.5 1.7 %collective-permute-start.20 = (f32[1,8,1024]{2,1,0:T(8,128)S(1)}, f32[1,8,1024]{2,1,0:T(8,128)S(1)}, u32[]{:S(2)}, u32[]{:S(2)}) collective-permute-start(f32[1,8,1024]{2,1,0:T(8,128)S(1)} %collective-permute-done.16.refs_2_), channel_id=1, source_target_pairs={{0,1},{1,0},{2,3},{3,2},{4,5},{5,4},{6,7},{7,6},{8,9},{9,8},{10,11... | collective-permute-start | bytes 98312 | tf_op jit(solution)/shard_map/ppermute | solution.py:306
  106.2 1.2 %collective-permute-start.21 = (f32[1,8,1024]{2,1,0:T(8,128)S(1)}, f32[1,8,1024]{2,1,0:T(8,128)S(1)}, u32[]{:S(2)}, u32[]{:S(2)}) collective-permute-start(f32[1,8,1024]{2,1,0:T(8,128)S(1)} %collective-permute-done.17.refs_3_), channel_id=1, source_target_pairs={{0,1},{1,0},{2,3},{3,2},{4,5},{5,4},{6,7},{7,6},{8,9},{9,8},{10,11... | collective-permute-start | bytes 98312 | tf_op jit(solution)/shard_map/ppermute | solution.py:306
  106.2 2.2 %copy-start.1 = (bf16[8,8192]{1,0:T(8,128)(2,1)}, bf16[8,8192]{1,0:T(8,128)(2,1)S(1)}, u32[]{:S(2)}) copy-start(bf16[8,8192]{1,0:T(8,128)(2,1)S(1)} %constant_dynamic-update-slice_fusion.8) | copy-start | bytes 393220
where the time goes:
time: 109 us; the launch traced here: 108 us
  waiting for transfers between devices  42.6 us (39%)
  starting transfers between devices  31.1 us (29%)
  Pallas kernels  30.2 us (28%)
  matrix products  2.06 us (2%)
  other arithmetic  1.15 us (1%)
    ppermute x20, waiting for transfers between devices, swap(): return lax.ppermute(x, 'ctx', [(s, s ^ mask) for s in range(size)])  38.5 us
    ppermute x20, starting transfers between devices, swap(): return lax.ppermute(x, 'ctx', [(s, s ^ mask) for s in range(size)])  20 us
    pallas_call x4, Pallas kernels, body(): pl.pallas_call(functools.partial(bulk_kernel, distance=p, first=first, pl...  10.9 us
    pallas_call x3, Pallas kernels, split(): pl.pallas_call(functools.partial(split_kernel, seats=seats), in_specs=[sc...  7.11 us
    all_to_all x1, starting transfers between devices, body(): mix = lax.all_to_all(packed, 'ctx', split_axis=0, concat_axis=0, tiled=True)  5.09 us
    pallas_call x1, Pallas kernels, body(): pl.pallas_call(functools.partial(embed_kernel, trees=trees, spots=spots),...  4.68 us
    all_to_all x1, waiting for transfers between devices, body(): lax.all_to_all(merged, 'ctx', split_axis=0, concat_axis=0, tiled=True, ax...  4.06 us
    all_to_all x1, starting transfers between devices, body(): lax.all_to_all(merged, 'ctx', split_axis=0, concat_axis=0, tiled=True, ax...  3.37 us
  transfers between devices with their start and end apart: 24, of which 11 were waited for; matrix products, arithmetic and copies ran while one was open for 3% of the time, Pallas kernels for 22%

commit v1 on v0

--- a/solution.py
+++ b/solution.py
@@ -17,7 +17,7 @@
 LANES = 128
 GROUP = KEY_HEADS
 HEAD_COLUMNS = PER_KEY * HEAD_WIDTH
-WEIGHT_PIECES = 8
+DIRECT = 8
 ROOM = 14 * 2**20
 STEP = 32
 ARRIVAL = (0, 2, 4, 3, 5, 6, 7, 1)
@@ -206,20 +206,9 @@
     out_ref[...] = mine_ref[...] + other_ref[...]
 
 
-def embed_kernel(pick_ref, mix_ref, weight_ref, out_ref, buffer, sems, *, trees, spots):
-    depth = weight_ref.shape[0] // WEIGHT_PIECES
-    copies = []
-    for i in range(WEIGHT_PIECES):
-        piece = pl.ds(i * depth, depth)
-        copies.append(
-            pltpu.make_async_copy(weight_ref.at[piece], buffer.at[piece], sems.at[i])
-        )
-    for c in copies:
-        c.start()
+def embed_kernel(pick_ref, mix_ref, weight_ref, out_ref, *, trees, spots):
     rows = dot(pick_ref[...], mix_ref[:, HEAD_COLUMNS:]).astype(bf16)
-    for c in copies:
-        c.wait()
-    join(rows, buffer, out_ref, trees=trees, spots=spots)
+    join(rows, weight_ref, out_ref, trees=trees, spots=spots)
 
 
 def feature_kernel(bit_ref, *refs, planes, feat, trees, spots):
@@ -255,6 +244,41 @@
         for s in range(slots):
             rows = rows + jnp.where(pick[:, s : s + 1] > 0.5, normed[s : s + 1, :], 0.0)
         out_ref[:, columns] = rows.astype(bf16)
+
+
+def bundle_kernel(merged_ref, mine_ref, other_ref, out_ref):
+    devices, owned, _ = merged_ref.shape
+    total = mine_ref[0] + other_ref[0]
+    high = total.astype(bf16)
+    low = (total - high.astype(f32)).astype(bf16)
+    for d in range(devices):
+        out_ref[d, 0:owned] = merged_ref[d]
+        out_ref[d, owned : owned + SLOTS] = high
+        out_ref[d, owned + SLOTS : owned + 2 * SLOTS] = low
+
+
+def last_kernel(bundle_ref, gain_ref, pick_ref, attended_ref, draft_ref, *, key_of):
+    devices, _, width = bundle_ref.shape
+    owned = attended_ref.shape[0]
+    joined = []
+    total = jnp.zeros((SLOTS, width), f32)
+    for d in range(devices):
+        columns = slice(key_of[d] * width, (key_of[d] + 1) * width)
+        attended_ref[:, columns] = bundle_ref[d, 0:owned]
+        high = bundle_ref[d, owned : owned + SLOTS].astype(f32)
+        low = bundle_ref[d, owned + SLOTS : owned + 2 * SLOTS].astype(f32)
+        joined.append(high + low)
+        total = total + joined[d] * joined[d]
+    total = jnp.sum(total, axis=1, keepdims=True)
+    factor = lax.rsqrt(total / (devices * width) + 1e-06)
+    pick = pick_ref[...]
+    for d in range(devices):
+        columns = slice(d * width, (d + 1) * width)
+        normed = joined[d] * factor * gain_ref[:, columns]
+        rows = jnp.zeros((pick.shape[0], width), f32)
+        for s in range(SLOTS):
+            rows = rows + jnp.where(pick[:, s : s + 1] > 0.5, normed[s : s + 1, :], 0.0)
+        draft_ref[:, columns] = rows.astype(bf16)
 
 
 def ancestors(parents):
@@ -325,30 +349,32 @@
             * len(seats),
             scratch_shapes=[pltpu.SemaphoreType.DMA((4 * len(seats),))],
             compiler_params=room,
+            cost_estimate=busy,
             name="split",
         )(place, *sources, *after)
 
-    slabs = list(split(ARRIVAL[1:5], ()))
-    slabs = list(split(ARRIVAL[:1], slabs[:1])) + slabs + list(split(ARRIVAL[5:], slabs[:1]))
-    after = slabs[-1]
+    first = list(split(ARRIVAL[1:3], ()))
+    second = list(split(ARRIVAL[3:6], first[:1]))
+    packed = pl.pallas_call(
+        functools.partial(mix_kernel, key_of=key_of),
+        in_specs=[stored, stored, outside],
+        out_specs=block,
+        out_shape=jax.ShapeDtypeStruct((size, owned, mixed), bf16),
+        scratch_shapes=[pltpu.SemaphoreType.DMA((2 * size,))],
+        compiler_params=room,
+        cost_estimate=busy,
+        name="pack",
+    )(leave(queries), leave(token_embed), second[0])
+    mix = lax.all_to_all(packed, "ctx", split_axis=0, concat_axis=0, tiled=True)
+    mix = pltpu.with_memory_space_constraint(mix.reshape(every_row, mixed), pltpu.VMEM)
+    third = list(split(ARRIVAL[6:] + ARRIVAL[:1], [packed]))
+    slabs = third[-1:] + first + second + third[:-1]
     for i, r in enumerate(ARRIVAL):
         if r:
             slabs[i] = swap(slabs[i], r)
     tree_kv = jnp.concatenate([s[positions:] for s in slabs], axis=0)
     tree_kv = jnp.pad(tree_kv, ((0, LANES - plane_rows), (0, 0)))
     slabs = [pltpu.with_memory_space_constraint(s, pltpu.VMEM) for s in slabs]
-
-    packed = pl.pallas_call(
-        functools.partial(mix_kernel, key_of=key_of),
-        in_specs=[stored, stored, outside],
-        out_specs=block,
-        out_shape=jax.ShapeDtypeStruct((size, owned, mixed), bf16),
-        scratch_shapes=[pltpu.SemaphoreType.DMA((2 * size,))],
-        compiler_params=room,
-        name="pack",
-    )(leave(queries), leave(token_embed), after)
-    mix = lax.all_to_all(packed, "ctx", split_axis=0, concat_axis=0, tiled=True)
-    mix = pltpu.with_memory_space_constraint(mix.reshape(every_row, mixed), pltpu.VMEM)
 
     closure = ancestors(parents)
     chosen = (accepted[:, None] == jnp.arange(nodes, dtype=jnp.int32)[None, :]).astype(f32)
@@ -381,7 +407,7 @@
 
     bits = size.bit_length() - 1
     inner = chunks.bit_length() - 1
-    order = [0, *range(inner, bits), *range(1, inner)]
+    order = list(range(bits))
     spots = tuple(
         sum(((d >> bit) & 1) << (bits - 1 - i) for i, bit in enumerate(order))
         for d in range(size)
@@ -395,17 +421,13 @@
 
     embed_part = pl.pallas_call(
         functools.partial(embed_kernel, trees=trees, spots=spots),
-        in_specs=[block, block, stored],
+        in_specs=[block] * 3,
         out_specs=block,
         out_shape=sums(size),
-        scratch_shapes=[
-            pltpu.VMEM((feat, model), bf16),
-            pltpu.SemaphoreType.DMA((WEIGHT_PIECES,)),
-        ],
         compiler_params=room,
         cost_estimate=busy,
         name="embed_join",
-    )(pick_rows, mix, leave(fc_embed))
+    )(pick_rows, mix, fc_embed)
 
     messages = pl.pallas_call(
         functools.partial(accepted_kernel, planes=planes, positions=positions, feat=feat),
@@ -447,30 +469,6 @@
                 compiler_params=room,
                 name="halve",
             )(bit_of(i + 1), keep, other)
-        else:
-            own = pl.pallas_call(
-                add_kernel,
-                in_specs=[block] * 2,
-                out_specs=block,
-                out_shape=sums(1),
-                compiler_params=room,
-                name="add",
-            )(keep, other)
-    joined = [own]
-    offsets = [0]
-    for bit in reversed(range(inner)):
-        joined = joined + [swap(x, 1 << bit) for x in joined]
-        offsets = offsets + [o ^ (1 << bit) for o in offsets]
-    joined = [pltpu.with_memory_space_constraint(x, pltpu.VMEM) for x in joined]
-    draft_input = pl.pallas_call(
-        functools.partial(norm_kernel, offsets=tuple(offsets)),
-        in_specs=[scalar] + [block] * (chunks + 2),
-        out_specs=block,
-        out_shape=jax.ShapeDtypeStruct((owned, model), bf16),
-        compiler_params=room,
-        name="norm",
-    )((me % chunks).astype(jnp.int32)[None], draft_gain[None, :], own_pick, *joined)
-
     rows = min(plane_rows, STEP)
     pieces = [(p, f) for p in [*range(1, planes), 0] for f in range(0, plane_rows, rows)]
     gathered = {}
@@ -500,6 +498,60 @@
         compiler_params=room,
         name="merge",
     )(*[gathered[k] for k in sorted(gathered)])
+    if chunks == GROUP:
+        bundle = pl.pallas_call(
+            bundle_kernel,
+            in_specs=[block] * 3,
+            out_specs=block,
+            out_shape=jax.ShapeDtypeStruct((GROUP, owned + 2 * SLOTS, HEAD_COLUMNS), bf16),
+            compiler_params=room,
+            name="bundle",
+        )(merged, keep, other)
+        bundle = lax.all_to_all(
+            bundle,
+            "ctx",
+            split_axis=0,
+            concat_axis=0,
+            tiled=True,
+            axis_index_groups=plane_groups,
+        )
+        bundle = pltpu.with_memory_space_constraint(bundle, pltpu.VMEM)
+        return tuple(
+            pl.pallas_call(
+                functools.partial(last_kernel, key_of=key_of),
+                in_specs=[block] * 3,
+                out_specs=[block] * 2,
+                out_shape=[jax.ShapeDtypeStruct((owned, model), bf16)] * 2,
+                compiler_params=room,
+                name="last",
+            )(bundle, draft_gain[None, :], own_pick)
+        )
+
+    own = pl.pallas_call(
+        add_kernel,
+        in_specs=[block] * 2,
+        out_specs=block,
+        out_shape=sums(1),
+        compiler_params=room,
+        name="add",
+    )(keep, other)
+    joined = [own]
+    offsets = [0]
+    masks = [(1 << bit,) for bit in reversed(range(inner)) if 1 << bit >= DIRECT]
+    masks.append(tuple(range(1, min(DIRECT, chunks))))
+    for mask in masks:
+        joined = joined + [swap(x, m) for m in mask for x in joined]
+        offsets = offsets + [o ^ m for m in mask for o in offsets]
+    joined = [pltpu.with_memory_space_constraint(x, pltpu.VMEM) for x in joined]
+    draft_input = pl.pallas_call(
+        functools.partial(norm_kernel, offsets=tuple(offsets)),
+        in_specs=[scalar] + [block] * (chunks + 2),
+        out_specs=block,
+        out_shape=jax.ShapeDtypeStruct((owned, model), bf16),
+        compiler_params=room,
+        name="norm",
+    )((me % chunks).astype(jnp.int32)[None], draft_gain[None, :], own_pick, *joined)
+
     by_seat = lax.all_to_all(
         merged,
         "ctx",

time: 109 us -> 94.5 us (0.87)
  waiting for transfers between devices: 42.6 us -> 32 us
  local copies, waits for them, and re-layouts: 0.33 us -> 4.43 us
  Pallas kernels: 30.2 us -> 26.2 us
  starting transfers between devices: 31.1 us -> 28.6 us
    ppermute x20 -> x13, waiting for transfers between devices: 38.5 us -> 24.9 us  [swap(): return lax.ppermute(x, 'ctx', [(s, s ^ mask) for s in range(size)])]
    ppermute x20 -> x13, starting transfers between devices: 20 us -> 14 us  [swap(): return lax.ppermute(x, 'ctx', [(s, s ^ mask) for s in range(size)])]
    unnamed x22 -> x23, local copies, waits for them, and re-layouts: 0.06 us -> 4.15 us
    pallas_call x1, Pallas kernels: 4.68 us -> 1.3 us  [body(): pl.pallas_call(functools.partial(embed_kernel, trees=trees, spots=spots),...]
    all_to_all x1, waiting for transfers between devices: 4.06 us -> 7.1 us  [body(): lax.all_to_all(bundle, 'ctx', split_axis=0, concat_axis=0, tiled=True, ax...]
    ppermute x2, starting transfers between devices: 2.6 us -> 4.95 us  [body(): arrived.append(lax.ppermute(messages[k], 'ctx', target))]
  transfers between devices with their start and end apart: 24 -> 17, of which waited for: 11 -> 6; matrix products, arithmetic and copies ran while one was open for 3% -> 2% of each run, Pallas kernels for 22% -> 20%
where the time goes in v1:
time: 94.5 us; the launch traced here: 94 us
  waiting for transfers between devices  32 us (34%)
  starting transfers between devices  28.6 us (30%)
  Pallas kernels  26.2 us (28%)
  local copies, waits for them, and re-layouts  4.43 us (5%)
  matrix products  1.31 us (1%)
  between operations  0.98 us (1%)
    ppermute x13, waiting for transfers between devices, swap(): return lax.ppermute(x, 'ctx', [(s, s ^ mask) for s in range(size)])  24.9 us
    ppermute x13, starting transfers between devices, swap(): return lax.ppermute(x, 'ctx', [(s, s ^ mask) for s in range(size)])  14 us
    pallas_call x4, Pallas kernels, body(): pl.pallas_call(functools.partial(bulk_kernel, distance=p, first=first, pl...  10.9 us
    all_to_all x1, waiting for transfers between devices, body(): lax.all_to_all(bundle, 'ctx', split_axis=0, concat_axis=0, tiled=True, ax...  7.1 us
    pallas_call x3, Pallas kernels, split(): pl.pallas_call(functools.partial(split_kernel, seats=seats), in_specs=[sc...  6.37 us
    all_to_all x1, starting transfers between devices, body(): mix = lax.all_to_all(packed, 'ctx', split_axis=0, concat_axis=0, tiled=True)  6.16 us
    ppermute x2, starting transfers between devices, body(): arrived.append(lax.ppermute(messages[k], 'ctx', target))  4.95 us
    unnamed x23, local copies, waits for them, and re-layouts  4.15 us
  transfers between devices with their start and end apart: 17, of which 6 were waited for; matrix products, arithmetic and copies ran while one was open for 2% of the time, Pallas kernels for 20%

profile of v1, /device:TPU:0, one launch (start us, length us, event | category | flops | bytes accessed | tf_op | source)
XLA Modules:
  0.0 94.0 jit_solution(9514859693872064086)
XLA Ops:
  0.7 2.5 %split.3 = (bf16[520,256]{1,0:T(8,128)(2,1)}, bf16[520,256]{1,0:T(8,128)(2,1)S(1)}) custom-call(s32[2]{0:T(128)S(1)} %pad_add_fusion.place_ref, bf16[512,1024]{1,0:T(8,128)(2,1)} %keys_ref.5, bf16[512,1024]{1,0:T(8,128)(2,1)} %values_ref.5, bf16[8,1024]{1,0:T(8,128)(2,1)} %tree_keys_ref.5, bf16[8,1024]{1,0:T(8,128)(2,1)} %tree_values_ref.5), custom_call_target="tpu_custom_call" | custom-call | flops 4000000000 | bytes 1000000 | tf_op jit(solution)/shard_map/split/pallas_call | solution.py:344
  3.2 3.1 %collective-permute-start = (bf16[520,256]{1,0:T(8,128)(2,1)}, bf16[520,256]{1,0:T(8,128)(2,1)S(1)}, u32[]{:S(2)}, u32[]{:S(2)}) collective-permute-start(bf16[520,256]{1,0:T(8,128)(2,1)} %get-tuple-element.20.refs_0_), channel_id=1, source_target_pairs={{0,2},{1,3},{2,0},{3,1},{4,6},{5,7},{6,4},{7,5},{8,10},{9,11},{10,... | collective-permute-start | bytes 798728 | tf_op jit(solution)/shard_map/ppermute | solution.py:330
  6.3 1.9 %split.4 = (bf16[520,256]{1,0:T(8,128)(2,1)S(1)}, bf16[520,256]{1,0:T(8,128)(2,1)S(1)}, bf16[520,256]{1,0:T(8,128)(2,1)S(1)}) custom-call(s32[2]{0:T(128)S(1)} %pad_add_fusion.place_ref, bf16[512,1024]{1,0:T(8,128)(2,1)} %keys_ref.5, bf16[512,1024]{1,0:T(8,128)(2,1)} %values_ref.5, bf16[8,1024]{1,0:T(8,128)(2,1)} %tree_keys_ref.5, ...), custom_call_target="tpu_custom_call" | custom-call | flops 4000000000 | bytes 1000000 | tf_op jit(solution)/shard_map/split/pallas_call | solution.py:344
  8.3 2.0 %pack.1.refs_0_ = bf16[16,8,1536]{2,1,0:T(8,128)(2,1)} custom-call(bf16[8,8192]{1,0:T(8,128)(2,1)} %query_ref.1, bf16[8,8192]{1,0:T(8,128)(2,1)} %embed_ref.1, bf16[520,256]{1,0:T(8,128)(2,1)S(1)} %get-tuple-element.21.after_ref), custom_call_target="tpu_custom_call" | custom-call | flops 4000000000 | bytes 1000000 | tf_op jit(solution)/shard_map/pack/pallas_call | solution.py:358
  10.3 6.2 %all-to-all-start = ((bf16[16,8,1536]{2,1,0:T(8,128)(2,1)}), bf16[16,8,1536]{2,1,0:T(8,128)(2,1)S(1)}, u32[]{:S(2)}, u32[]{:S(2)}) async-start(bf16[16,8,1536]{2,1,0:T(8,128)(2,1)} %pack.1.refs_0_), calls=%async_computation | async-start | bytes 786432 | tf_op jit(solution)/shard_map/all_to_all | solution.py:368
  16.5 1.9 %collective-permute-start.1 = (bf16[520,256]{1,0:T(8,128)(2,1)S(1)}, bf16[520,256]{1,0:T(8,128)(2,1)S(1)}, u32[]{:S(2)}, u32[]{:S(2)}) collective-permute-start(bf16[520,256]{1,0:T(8,128)(2,1)S(1)} %get-tuple-element.23), channel_id=1, source_target_pairs={{0,4},{1,5},{2,6},{3,7},{4,0},{5,1},{6,2},{7,3},{8,12},{9,13},{10,... | collective-permute-start | bytes 798728 | tf_op jit(solution)/shard_map/ppermute | solution.py:330
  18.4 2.4 %collective-permute-start.4 = (bf16[520,256]{1,0:T(8,128)(2,1)S(1)}, bf16[520,256]{1,0:T(8,128)(2,1)S(1)}, u32[]{:S(2)}, u32[]{:S(2)}) collective-permute-start(bf16[520,256]{1,0:T(8,128)(2,1)S(1)} %get-tuple-element.25), channel_id=1, source_target_pairs={{0,6},{1,7},{2,4},{3,5},{4,2},{5,3},{6,0},{7,1},{8,14},{9,15},{10,... | collective-permute-start | bytes 798728 | tf_op jit(solution)/shard_map/ppermute | solution.py:330
  20.8 1.9 %split.5 = (bf16[520,256]{1,0:T(8,128)(2,1)S(1)}, bf16[520,256]{1,0:T(8,128)(2,1)S(1)}, bf16[520,256]{1,0:T(8,128)(2,1)S(1)}) custom-call(s32[2]{0:T(128)S(1)} %pad_add_fusion.place_ref, bf16[512,1024]{1,0:T(8,128)(2,1)} %keys_ref.5, bf16[512,1024]{1,0:T(8,128)(2,1)} %values_ref.5, bf16[8,1024]{1,0:T(8,128)(2,1)} %tree_keys_ref.5, ...), custom_call_target="tpu_custom_call" | custom-call | flops 4000000000 | bytes 1000000 | tf_op jit(solution)/shard_map/split/pallas_call | solution.py:344
  22.8 0.7 copy-done.3
  23.5 0.2 convolution_minimum_fusion.2
  23.8 0.3 convolution_minimum_fusion
  24.1 0.1 fusion.20
  24.2 0.1 fusion.18
  24.4 0.1 broadcast_multiply_fusion
  24.5 0.1 mul.73
  24.7 0.1 multiply_reduce_fusion
  24.8 0.1 convert_element_type.46.refs_10_.pick_ref
  24.9 0.1 fusion.refs_9_
  25.0 0.2 fusion.7.refs_9_
  25.3 0.3 collective-permute-start.5
  25.6 6.6 %collective-permute-done.1.refs_2_ = bf16[520,256]{1,0:T(8,128)(2,1)S(1)} collective-permute-done((bf16[520,256]{1,0:T(8,128)(2,1)S(1)}, bf16[520,256]{1,0:T(8,128)(2,1)S(1)}, u32[]{:S(2)}, u32[]{:S(2)}) %collective-permute-start.1) | collective-permute-done | bytes 266272 | tf_op jit(solution)/shard_map/ppermute | solution.py:330
  32.2 4.5 %collective-permute-done.3.refs_4_ = bf16[520,256]{1,0:T(8,128)(2,1)S(1)} collective-permute-done((bf16[520,256]{1,0:T(8,128)(2,1)S(1)}, bf16[520,256]{1,0:T(8,128)(2,1)S(1)}, u32[]{:S(2)}, u32[]{:S(2)}) %collective-permute-start.3) | collective-permute-done | bytes 266272 | tf_op jit(solution)/shard_map/ppermute | solution.py:330
  36.8 7.7 %collective-permute-done.4.refs_5_ = bf16[520,256]{1,0:T(8,128)(2,1)S(1)} collective-permute-done((bf16[520,256]{1,0:T(8,128)(2,1)S(1)}, bf16[520,256]{1,0:T(8,128)(2,1)S(1)}, u32[]{:S(2)}, u32[]{:S(2)}) %collective-permute-start.4) | collective-permute-done | bytes 266272 | tf_op jit(solution)/shard_map/ppermute | solution.py:330
  44.5 4.6 %collective-permute-done.5.refs_6_ = bf16[520,256]{1,0:T(8,128)(2,1)S(1)} collective-permute-done((bf16[520,256]{1,0:T(8,128)(2,1)}, bf16[520,256]{1,0:T(8,128)(2,1)S(1)}, u32[]{:S(2)}, u32[]{:S(2)}) %collective-permute-start.5) | collective-permute-done | bytes 266272 | tf_op jit(solution)/shard_map/ppermute | solution.py:330
  49.1 2.0 %accepted.1 = (f32[16,640]{1,0:T(8,128)S(1)}, f32[16,640]{1,0:T(8,128)S(1)}) custom-call(s32[2]{0:T(128)S(1)} %pad_add_fusion.place_ref, bf16[128,1536]{1,0:T(8,128)(2,1)S(1)} %bitcast.44, bf16[520,256]{1,0:T(8,128)(2,1)S(1)} %get-tuple-element.22.refs_0_, bf16[520,256]{1,0:T(8,128)(2,1)S(1)} %collective-permute-done.refs_1_, ...), custom_call_target="tpu_custom_call" | custom-call | flops 4000000000 | bytes 1000000 | tf_op jit(solution)/shard_map/accepted/pallas_call | solution.py:432
  51.1 0.8 collective-permute-start.9
  51.9 4.2 %collective-permute-start.10 = (f32[16,640]{1,0:T(8,128)S(1)}, f32[16,640]{1,0:T(8,128)S(1)}, u32[]{:S(2)}, u32[]{:S(2)}) collective-permute-start(f32[16,640]{1,0:T(8,128)S(1)} %get-tuple-element.29), channel_id=1, source_target_pairs={{0,1},{1,9},{2,3},{3,11},{4,5},{5,13},{6,7},{7,15},{8,0},{9,8},{10... | collective-permute-start | bytes 122888 | tf_op jit(solution)/shard_map/ppermute | solution.py:449
  56.1 3.4 %copy-done.1 = bf16[512,8192]{1,0:T(8,128)(2,1)S(1)} copy-done((bf16[512,8192]{1,0:T(8,128)(2,1)S(1)}, bf16[512,8192]{1,0:T(8,128)(2,1)}, u32[]{:S(2)}) %copy-start.1) | copy-done | bytes 8388632
  59.4 1.3 %embed_join.1.refs_3_ = f32[16,8,1024]{2,1,0:T(8,128)S(1)} custom-call(bf16[16,128]{1,0:T(8,128)(2,1)S(1)} %convert_element_type.46.refs_10_.pick_ref, bf16[128,1536]{1,0:T(8,128)(2,1)S(1)} %bitcast.45, bf16[512,8192]{1,0:T(8,128)(2,1)S(1)} %copy-done.1), custom_call_target="tpu_custom_call" | custom-call | flops 4000000000 | bytes 1000000 | tf_op jit(solution)/shard_map/embed_join/pallas_call | solution.py:422
  60.8 1.3 %feature_join.1 = (f32[8,8,1024]{2,1,0:T(8,128)S(1)}, f32[8,8,1024]{2,1,0:T(8,128)S(1)}) custom-call(s32[1]{0:T(128)} %bitcast.11.bit_ref, f32[16,640]{1,0:T(8,128)S(1)} %collective-permute-done.9.refs_0_, f32[16,640]{1,0:T(8,128)S(1)} %collective-permute-done.10.refs_1_, bf16[512,8192]{1,0:T(8,128)(2,1)S(1)} %bitcast.43, f32[16,8,1024]{2,1,0:T(8,128)S(1)} %embed_join.1.refs_3_), custom_call_target="tpu_custom_call" | custom-call | tf_op jit(solution)/shard_map/feature_join/pallas_call | solution.py:451
  62.1 0.1 collective-permute-start.11
  62.2 2.7 %shard_map.132 = bf16[32,1152]{1,0:T(8,128)(2,1)S(1)} custom-call(s32[2]{0:T(128)S(1)} %pad_add_fusion.place_ref, bf16[128,1536]{1,0:T(8,128)(2,1)S(1)} %bitcast.46, bf16[520,256]{1,0:T(8,128)(2,1)S(1)} %get-tuple-element.22.refs_0_, bf16[520,256]{1,0:T(8,128)(2,1)S(1)} %collective-permute-done.refs_1_, bf16[520,256]{1,0:T(8,128)(2,1)S(1)} %collective-permute-done.1.refs_2_, ...), custom_call_target="tpu_custom_call" | custom-call | flops 4000000000 | bytes 1000000 | tf_op jit(solution)/shard_map/pallas_call | solution.py:476
  64.9 1.0 %collective-permute-start.7 = (bf16[32,1152]{1,0:T(8,128)(2,1)S(1)}, bf16[32,1152]{1,0:T(8,128)(2,1)S(1)}, u32[]{:S(2)}, u32[]{:S(2)}) collective-permute-start(bf16[32,1152]{1,0:T(8,128)(2,1)S(1)} %shard_map.132), channel_id=1, source_target_pairs={{0,8},{1,9},{2,10},{3,11},{4,12},{5,13},{6,14},{7,15},{8,0},{9,1},... | collective-permute-start | bytes 221192 | tf_op jit(solution)/shard_map/ppermute | solution.py:330
  65.9 0.6 collective-permute-start.12
  66.5 2.7 %shard_map.134 = bf16[32,1152]{1,0:T(8,128)(2,1)S(1)} custom-call(s32[2]{0:T(128)S(1)} %pad_add_fusion.place_ref, bf16[128,1536]{1,0:T(8,128)(2,1)S(1)} %bitcast.47, bf16[520,256]{1,0:T(8,128)(2,1)S(1)} %get-tuple-element.22.refs_0_, bf16[520,256]{1,0:T(8,128)(2,1)S(1)} %collective-permute-done.refs_1_, bf16[520,256]{1,0:T(8,128)(2,1)S(1)} %collective-permute-done.1.refs_2_, ...), custom_call_target="tpu_custom_call" | custom-call | flops 4000000000 | bytes 1000000 | tf_op jit(solution)/shard_map/pallas_call | solution.py:476
  69.2 2.1 %collective-permute-start.8 = (bf16[32,1152]{1,0:T(8,128)(2,1)S(1)}, bf16[32,1152]{1,0:T(8,128)(2,1)S(1)}, u32[]{:S(2)}, u32[]{:S(2)}) collective-permute-start(bf16[32,1152]{1,0:T(8,128)(2,1)S(1)} %shard_map.134), channel_id=1, source_target_pairs={{0,8},{1,9},{2,10},{3,11},{4,12},{5,13},{6,14},{7,15},{8,0},{9,1},... | collective-permute-start | bytes 221192 | tf_op jit(solution)/shard_map/ppermute | solution.py:330
  71.4 0.6 collective-permute-start.13
  72.0 2.7 %shard_map.131.refs_0_ = bf16[32,1152]{1,0:T(8,128)(2,1)S(1)} custom-call(s32[2]{0:T(128)S(1)} %pad_add_fusion.place_ref, bf16[128,1536]{1,0:T(8,128)(2,1)S(1)} %bitcast.48, bf16[520,256]{1,0:T(8,128)(2,1)S(1)} %get-tuple-element.22.refs_0_, bf16[520,256]{1,0:T(8,128)(2,1)S(1)} %collective-permute-done.refs_1_, ...), custom_call_target="tpu_custom_call" | custom-call | flops 4000000000 | bytes 1000000 | tf_op jit(solution)/shard_map/pallas_call | solution.py:476
  74.7 1.4 %collective-permute-done.13.other_ref = f32[2,8,1024]{2,1,0:T(8,128)S(1)} collective-permute-done((f32[2,8,1024]{2,1,0:T(8,128)S(1)}, f32[2,8,1024]{2,1,0:T(8,128)S(1)}, u32[]{:S(2)}, u32[]{:S(2)}) %collective-permute-start.13) | collective-permute-done | bytes 65568 | tf_op jit(solution)/shard_map/ppermute | solution.py:330
  76.1 1.9 %collective-permute-start.14 = (f32[1,8,1024]{2,1,0:T(8,128)S(1)}, f32[1,8,1024]{2,1,0:T(8,128)S(1)}, u32[]{:S(2)}, u32[]{:S(2)}) collective-permute-start(f32[1,8,1024]{2,1,0:T(8,128)S(1)} %get-tuple-element.37), channel_id=1, source_target_pairs={{0,8},{1,9},{2,10},{3,11},{4,12},{5,13},{6,14},{7,15},{8,0},{9,1},... | collective-permute-start | bytes 98312 | tf_op jit(solution)/shard_map/ppermute | solution.py:330
  78.0 2.7 %shard_map.133.refs_2_ = bf16[32,1152]{1,0:T(8,128)(2,1)S(1)} custom-call(s32[2]{0:T(128)S(1)} %pad_add_fusion.place_ref, bf16[128,1536]{1,0:T(8,128)(2,1)S(1)} %bitcast.49, bf16[520,256]{1,0:T(8,128)(2,1)S(1)} %get-tuple-element.22.refs_0_, bf16[520,256]{1,0:T(8,128)(2,1)S(1)} %collective-permute-done.refs_1_, ...), custom_call_target="tpu_custom_call" | custom-call | flops 4000000000 | bytes 1000000 | tf_op jit(solution)/shard_map/pallas_call | solution.py:476
  80.8 0.5 merge.1.merged_ref
  81.4 0.8 bundle.1
  82.1 3.5 %all-to-all-start.1 = ((bf16[8,24,1024]{2,1,0:T(8,128)(2,1)}), bf16[8,24,1024]{2,1,0:T(8,128)(2,1)S(1)}, u32[]{:S(2)}, u32[]{:S(2)}) async-start(bf16[8,24,1024]{2,1,0:T(8,128)(2,1)} %bundle.1), calls=%async_computation.1 | async-start | bytes 786432 | tf_op jit(solution)/shard_map/all_to_all | solution.py:510
  85.6 0.1 reduce_sum.12
  85.7 0.2 fusion.19.pick_ref
  85.9 7.1 %all-to-all-done.1.bundle_ref = bf16[8,24,1024]{2,1,0:T(8,128)(2,1)S(1)} async-done(((bf16[8,24,1024]{2,1,0:T(8,128)(2,1)}), bf16[8,24,1024]{2,1,0:T(8,128)(2,1)S(1)}, u32[]{:S(2)}, u32[]{:S(2)}) %all-to-all-start.1) | async-done | bytes 393248 | tf_op jit(solution)/shard_map/all_to_all | solution.py:510
  93.0 1.0 %last.1 = (bf16[8,8192]{1,0:T(8,128)(2,1)}, bf16[8,8192]{1,0:T(8,128)(2,1)}) custom-call(bf16[8,24,1024]{2,1,0:T(8,128)(2,1)S(1)} %all-to-all-done.1.bundle_ref, f32[1,8192]{1,0:T(1,128)S(1)} %bitcast.50, f32[8,8]{1,0:T(8,128)S(1)} %fusion.19.pick_ref), custom_call_target="tpu_custom_call" | custom-call | tf_op jit(solution)/shard_map/last/pallas_call | solution.py:520
  (51 shorter events, 0.6 us)
Async XLA Ops:
  3.2 22.1 %collective-permute-start = (bf16[520,256]{1,0:T(8,128)(2,1)}, bf16[520,256]{1,0:T(8,128)(2,1)S(1)}, u32[]{:S(2)}, u32[]{:S(2)}) collective-permute-start(bf16[520,256]{1,0:T(8,128)(2,1)} %get-tuple-element.20.refs_0_), channel_id=1, source_target_pairs={{0,2},{1,3},{2,0},{3,1},{4,6},{5,7},{6,4},{7,5},{8,10},{9,11},{10,... | collective-permute-start | bytes 798728 | tf_op jit(solution)/shard_map/ppermute | solution.py:330
  8.2 24.0 %collective-permute-start.2 = (bf16[520,256]{1,0:T(8,128)(2,1)S(1)}, bf16[520,256]{1,0:T(8,128)(2,1)S(1)}, u32[]{:S(2)}, u32[]{:S(2)}) collective-permute-start(bf16[520,256]{1,0:T(8,128)(2,1)S(1)} %get-tuple-element.21.after_ref), channel_id=1, source_target_pairs={{0,3},{1,2},{2,1},{3,0},{4,7},{5,6},{6,5},{7,4},{8,11},{9,10},{10,... | collective-permute-start | bytes 798728 | tf_op jit(solution)/shard_map/ppermute | solution.py:330
  10.3 13.2 %copy-start.4 = (s32[2,64]{1,0:T(2,128)S(1)}, s32[2,64]{1,0:T(2,128)}, u32[]{:S(2)}) copy-start(s32[2,64]{1,0:T(2,128)} %param.21) | copy-start | bytes 1540
  10.3 13.7 %copy-start.5 = (s32[2]{0:T(128)S(1)}, s32[2]{0:T(128)}, u32[]{:S(2)}) copy-start(s32[2]{0:T(128)} %param.22) | copy-start | bytes 28
  10.3 38.7 %all-to-all-start = ((bf16[16,8,1536]{2,1,0:T(8,128)(2,1)}), bf16[16,8,1536]{2,1,0:T(8,128)(2,1)S(1)}, u32[]{:S(2)}, u32[]{:S(2)}) async-start(bf16[16,8,1536]{2,1,0:T(8,128)(2,1)} %pack.1.refs_0_), calls=%async_computation | async-start | bytes 786432 | tf_op jit(solution)/shard_map/all_to_all | solution.py:368
  16.5 15.7 %collective-permute-start.1 = (bf16[520,256]{1,0:T(8,128)(2,1)S(1)}, bf16[520,256]{1,0:T(8,128)(2,1)S(1)}, u32[]{:S(2)}, u32[]{:S(2)}) collective-permute-start(bf16[520,256]{1,0:T(8,128)(2,1)S(1)} %get-tuple-element.23), channel_id=1, source_target_pairs={{0,4},{1,5},{2,6},{3,7},{4,0},{5,1},{6,2},{7,3},{8,12},{9,13},{10,... | collective-permute-start | bytes 798728 | tf_op jit(solution)/shard_map/ppermute | solution.py:330
  18.4 18.3 %collective-permute-start.3 = (bf16[520,256]{1,0:T(8,128)(2,1)S(1)}, bf16[520,256]{1,0:T(8,128)(2,1)S(1)}, u32[]{:S(2)}, u32[]{:S(2)}) collective-permute-start(bf16[520,256]{1,0:T(8,128)(2,1)S(1)} %get-tuple-element.24), channel_id=1, source_target_pairs={{0,5},{1,4},{2,7},{3,6},{4,1},{5,0},{6,3},{7,2},{8,13},{9,12},{10,... | collective-permute-start | bytes 798728 | tf_op jit(solution)/shard_map/ppermute | solution.py:330
  18.4 26.1 %collective-permute-start.4 = (bf16[520,256]{1,0:T(8,128)(2,1)S(1)}, bf16[520,256]{1,0:T(8,128)(2,1)S(1)}, u32[]{:S(2)}, u32[]{:S(2)}) collective-permute-start(bf16[520,256]{1,0:T(8,128)(2,1)S(1)} %get-tuple-element.25), channel_id=1, source_target_pairs={{0,6},{1,7},{2,4},{3,5},{4,2},{5,3},{6,0},{7,1},{8,14},{9,15},{10,... | collective-permute-start | bytes 798728 | tf_op jit(solution)/shard_map/ppermute | solution.py:330
  22.8 0.7 copy-start.3
  23.5 1.8 %copy-start.2 = (bf16[520,256]{1,0:T(8,128)(2,1)}, bf16[520,256]{1,0:T(8,128)(2,1)S(1)}, u32[]{:S(2)}) copy-start(bf16[520,256]{1,0:T(8,128)(2,1)S(1)} %get-tuple-element.27) | copy-start | bytes 798724
  25.3 23.8 %collective-permute-start.5 = (bf16[520,256]{1,0:T(8,128)(2,1)}, bf16[520,256]{1,0:T(8,128)(2,1)S(1)}, u32[]{:S(2)}, u32[]{:S(2)}) collective-permute-start(bf16[520,256]{1,0:T(8,128)(2,1)} %copy-done.3), channel_id=1, source_target_pairs={{0,7},{1,6},{2,5},{3,4},{4,3},{5,2},{6,1},{7,0},{8,15},{9,14},{10,... | collective-permute-start | bytes 798728 | tf_op jit(solution)/shard_map/ppermute | solution.py:330
  32.2 16.9 %collective-permute-start.6 = (bf16[520,256]{1,0:T(8,128)(2,1)}, bf16[520,256]{1,0:T(8,128)(2,1)S(1)}, u32[]{:S(2)}, u32[]{:S(2)}) collective-permute-start(bf16[520,256]{1,0:T(8,128)(2,1)} %copy-done.2), channel_id=1, source_target_pairs={{0,1},{1,0},{2,3},{3,2},{4,5},{5,4},{6,7},{7,6},{8,9},{9,8},{10,11... | collective-permute-start | bytes 798728 | tf_op jit(solution)/shard_map/ppermute | solution.py:330
  49.1 11.7 %slice-start = ((s8[8388608]{0:T(1024)(128)(4,1)}), s8[4194304]{0:T(1024)(128)(4,1)S(1)}, s32[]{:S(2)}) async-start(s8[8388608]{0:T(1024)(128)(4,1)} %bitcast.42), calls=%async_computation.2 | async-start | bytes 8388608
  51.1 9.7 %slice-start.1 = ((s8[8388608]{0:T(1024)(128)(4,1)}), s8[4194304]{0:T(1024)(128)(4,1)S(1)}, s32[]{:S(2)}) async-start(s8[8388608]{0:T(1024)(128)(4,1)} %bitcast.42), calls=%async_computation.3 | async-start | bytes 8388608
  51.1 9.6 %collective-permute-start.9 = (f32[16,640]{1,0:T(8,128)S(1)}, f32[16,640]{1,0:T(8,128)S(1)}, u32[]{:S(2)}, u32[]{:S(2)}) collective-permute-start(f32[16,640]{1,0:T(8,128)S(1)} %get-tuple-element.28.refs_10_), channel_id=1, source_target_pairs={{0,0},{1,8},{2,2},{3,10},{4,4},{5,12},{6,6},{7,14},{8,1},{9,9},{10... | collective-permute-start | bytes 122888 | tf_op jit(solution)/shard_map/ppermute | solution.py:449
  51.9 8.8 %collective-permute-start.10 = (f32[16,640]{1,0:T(8,128)S(1)}, f32[16,640]{1,0:T(8,128)S(1)}, u32[]{:S(2)}, u32[]{:S(2)}) collective-permute-start(f32[16,640]{1,0:T(8,128)S(1)} %get-tuple-element.29), channel_id=1, source_target_pairs={{0,1},{1,9},{2,3},{3,11},{4,5},{5,13},{6,7},{7,15},{8,0},{9,8},{10... | collective-permute-start | bytes 122888 | tf_op jit(solution)/shard_map/ppermute | solution.py:449
  56.1 3.4 %copy-start.1 = (bf16[512,8192]{1,0:T(8,128)(2,1)S(1)}, bf16[512,8192]{1,0:T(8,128)(2,1)}, u32[]{:S(2)}) copy-start(bf16[512,8192]{1,0:T(8,128)(2,1)} %weight_ref.1) | copy-start | bytes 25165828
  62.1 3.8 %collective-permute-start.11 = (f32[8,8,1024]{2,1,0:T(8,128)S(1)}, f32[8,8,1024]{2,1,0:T(8,128)S(1)}, u32[]{:S(2)}, u32[]{:S(2)}) collective-permute-start(f32[8,8,1024]{2,1,0:T(8,128)S(1)} %get-tuple-element.31), channel_id=1, source_target_pairs={{0,1},{1,0},{2,3},{3,2},{4,5},{5,4},{6,7},{7,6},{8,9},{9,8},{10,11... | collective-permute-start | bytes 786440 | tf_op jit(solution)/shard_map/ppermute | solution.py:330
  64.9 15.9 %collective-permute-start.7 = (bf16[32,1152]{1,0:T(8,128)(2,1)S(1)}, bf16[32,1152]{1,0:T(8,128)(2,1)S(1)}, u32[]{:S(2)}, u32[]{:S(2)}) collective-permute-start(bf16[32,1152]{1,0:T(8,128)(2,1)S(1)} %shard_map.132), channel_id=1, source_target_pairs={{0,8},{1,9},{2,10},{3,11},{4,12},{5,13},{6,14},{7,15},{8,0},{9,1},... | collective-permute-start | bytes 221192 | tf_op jit(solution)/shard_map/ppermute | solution.py:330
  65.9 5.4 %collective-permute-start.12 = (f32[4,8,1024]{2,1,0:T(8,128)S(1)}, f32[4,8,1024]{2,1,0:T(8,128)S(1)}, u32[]{:S(2)}, u32[]{:S(2)}) collective-permute-start(f32[4,8,1024]{2,1,0:T(8,128)S(1)} %get-tuple-element.33), channel_id=1, source_target_pairs={{0,2},{1,3},{2,0},{3,1},{4,6},{5,7},{6,4},{7,5},{8,10},{9,11},{10,... | collective-permute-start | bytes 393224 | tf_op jit(solution)/shard_map/ppermute | solution.py:330
  69.2 11.5 %collective-permute-start.8 = (bf16[32,1152]{1,0:T(8,128)(2,1)S(1)}, bf16[32,1152]{1,0:T(8,128)(2,1)S(1)}, u32[]{:S(2)}, u32[]{:S(2)}) collective-permute-start(bf16[32,1152]{1,0:T(8,128)(2,1)S(1)} %shard_map.134), channel_id=1, source_target_pairs={{0,8},{1,9},{2,10},{3,11},{4,12},{5,13},{6,14},{7,15},{8,0},{9,1},... | collective-permute-start | bytes 221192 | tf_op jit(solution)/shard_map/ppermute | solution.py:330
  71.4 4.8 %collective-permute-start.13 = (f32[2,8,1024]{2,1,0:T(8,128)S(1)}, f32[2,8,1024]{2,1,0:T(8,128)S(1)}, u32[]{:S(2)}, u32[]{:S(2)}) collective-permute-start(f32[2,8,1024]{2,1,0:T(8,128)S(1)} %get-tuple-element.35), channel_id=1, source_target_pairs={{0,4},{1,5},{2,6},{3,7},{4,0},{5,1},{6,2},{7,3},{8,12},{9,13},{10,... | collective-permute-start | bytes 196616 | tf_op jit(solution)/shard_map/ppermute | solution.py:330
  76.1 16.9 %copy-start = (f32[8192]{0:T(1024)S(1)}, f32[8192]{0:T(1024)}, u32[]{:S(2)}) copy-start(f32[8192]{0:T(1024)} %param.20) | copy-start | bytes 98308
  76.1 5.2 %collective-permute-start.14 = (f32[1,8,1024]{2,1,0:T(8,128)S(1)}, f32[1,8,1024]{2,1,0:T(8,128)S(1)}, u32[]{:S(2)}, u32[]{:S(2)}) collective-permute-start(f32[1,8,1024]{2,1,0:T(8,128)S(1)} %get-tuple-element.37), channel_id=1, source_target_pairs={{0,8},{1,9},{2,10},{3,11},{4,12},{5,13},{6,14},{7,15},{8,0},{9,1},... | collective-permute-start | bytes 98312 | tf_op jit(solution)/shard_map/ppermute | solution.py:330
  82.1 10.8 %all-to-all-start.1 = ((bf16[8,24,1024]{2,1,0:T(8,128)(2,1)}), bf16[8,24,1024]{2,1,0:T(8,128)(2,1)S(1)}, u32[]{:S(2)}, u32[]{:S(2)}) async-start(bf16[8,24,1024]{2,1,0:T(8,128)(2,1)} %bundle.1), calls=%async_computation.1 | async-start | bytes 786432 | tf_op jit(solution)/shard_map/all_to_all | solution.py:510

commit v2 on v1

--- a/solution.py
+++ b/solution.py
@@ -20,7 +20,7 @@
 DIRECT = 8
 ROOM = 14 * 2**20
 STEP = 32
-ARRIVAL = (0, 2, 4, 3, 5, 6, 7, 1)
+ARRIVAL = (0, 4, 2, 5, 3, 6, 7, 1)
 NEGATIVE = -1e30
 LOG2_SCALE = HEAD_WIDTH**-0.5 * math.log2(math.e)
 
@@ -64,24 +64,27 @@
     slabs = refs[:GROUP]
     tree_ref, bias_ref = refs[GROUP : GROUP + 2]
     out_ref = refs[-1]
-    step = out_ref.shape[0]
-    start = pl.multiple_of((place_ref[0] ^ distance) * plane_rows + first, step)
-    q = stack_heads(mix_ref[pl.ds(start, step), 0:HEAD_COLUMNS])
-    bias = jnp.concatenate([bias_ref[pl.ds(start, step), :]] * PER_KEY, axis=0)
-    out, lse = attend(q, slabs, positions, tree_ref, bias)
-    lane = lax.broadcasted_iota(jnp.int32, (step, LANES), 1)
-    stats = jnp.zeros((step, LANES), f32)
-    for h in range(PER_KEY):
-        part = slice(h * step, (h + 1) * step)
-        column = slice(h * HEAD_WIDTH, (h + 1) * HEAD_WIDTH)
-        out_ref[:, column] = out[part].astype(bf16)
-        high = lse[part].astype(bf16).astype(f32)
-        middle = (lse[part] - high).astype(bf16).astype(f32)
-        low = lse[part] - high - middle
-        stats = jnp.where(lane == h, high, stats)
-        stats = jnp.where(lane == PER_KEY + h, middle, stats)
-        stats = jnp.where(lane == 2 * PER_KEY + h, low, stats)
-    out_ref[:, HEAD_COLUMNS : HEAD_COLUMNS + LANES] = stats.astype(bf16)
+    rows = out_ref.shape[0]
+    step = min(rows, STEP)
+    for tile in range(0, rows, step):
+        start = pl.multiple_of((place_ref[0] ^ distance) * plane_rows + first + tile, step)
+        q = stack_heads(mix_ref[pl.ds(start, step), 0:HEAD_COLUMNS])
+        bias = jnp.concatenate([bias_ref[pl.ds(start, step), :]] * PER_KEY, axis=0)
+        out, lse = attend(q, slabs, positions, tree_ref, bias)
+        lane = lax.broadcasted_iota(jnp.int32, (step, LANES), 1)
+        stats = jnp.zeros((step, LANES), f32)
+        piece = slice(tile, tile + step)
+        for h in range(PER_KEY):
+            part = slice(h * step, (h + 1) * step)
+            column = slice(h * HEAD_WIDTH, (h + 1) * HEAD_WIDTH)
+            out_ref[piece, column] = out[part].astype(bf16)
+            high = lse[part].astype(bf16).astype(f32)
+            middle = (lse[part] - high).astype(bf16).astype(f32)
+            low = lse[part] - high - middle
+            stats = jnp.where(lane == h, high, stats)
+            stats = jnp.where(lane == PER_KEY + h, middle, stats)
+            stats = jnp.where(lane == 2 * PER_KEY + h, low, stats)
+        out_ref[piece, HEAD_COLUMNS : HEAD_COLUMNS + LANES] = stats.astype(bf16)
 
 
 def accepted_kernel(place_ref, mix_ref, *refs, planes, positions, feat):
@@ -335,6 +338,7 @@
         return pltpu.with_memory_space_constraint(x, pltpu.HBM)
 
     place = jnp.stack([plane, seat]).astype(jnp.int32)
+    here = plane.astype(jnp.int32)[None]
     sources = [
         leave(x)
         for x in (prefix_key_heads, prefix_value_heads, tree_key_heads, tree_value_heads)
@@ -438,7 +442,7 @@
         compiler_params=room,
         cost_estimate=busy,
         name="accepted",
-    )(place, mix, *slabs, tree_kv, bias_picked, pick_rows)
+    )(here, mix, *slabs, tree_kv, bias_picked, pick_rows)
     arrived = []
     for k in range(planes):
         target = [
@@ -486,7 +490,7 @@
             out_shape=jax.ShapeDtypeStruct((rows, HEAD_COLUMNS + LANES), bf16),
             compiler_params=room,
             cost_estimate=busy,
-        )(place, mix, *slabs, tree_kv, bias, messages[0])
+        )(here, mix, *slabs, tree_kv, bias, messages[0])
         if p:
             out = swap(out, GROUP * p)
         gathered[first, p] = pltpu.with_memory_space_constraint(out, pltpu.VMEM)

time: 94.5 us -> 90.2 us (0.954)
  waiting for transfers between devices: 32 us -> 28.5 us
  Pallas kernels: 26.2 us -> 23.5 us
  starting transfers between devices: 28.6 us -> 30.5 us
    ppermute x13, waiting for transfers between devices: 24.9 us -> 21.3 us  [swap(): return lax.ppermute(x, 'ctx', [(s, s ^ mask) for s in range(size)])]
    pallas_call x4, Pallas kernels: 10.9 us -> 8.71 us  [body(): pl.pallas_call(functools.partial(bulk_kernel, distance=p, first=first, pl...]
    ppermute x13, starting transfers between devices: 14 us -> 15.7 us  [swap(): return lax.ppermute(x, 'ctx', [(s, s ^ mask) for s in range(size)])]
  transfers between devices with their start and end apart: 17 -> 17, of which waited for: 6 -> 5; matrix products, arithmetic and copies ran while one was open for 2% -> 2% of each run, Pallas kernels for 20% -> 18%
where the time goes in v2:
time: 90.2 us; the launch traced here: 89.7 us
  starting transfers between devices  30.5 us (34%)
  waiting for transfers between devices  28.5 us (32%)
  Pallas kernels  23.5 us (26%)
  local copies, waits for them, and re-layouts  4.43 us (5%)
  matrix products  1.31 us (1%)
  between operations  1.01 us (1%)
    ppermute x13, waiting for transfers between devices, swap(): return lax.ppermute(x, 'ctx', [(s, s ^ mask) for s in range(size)])  21.3 us
    ppermute x13, starting transfers between devices, swap(): return lax.ppermute(x, 'ctx', [(s, s ^ mask) for s in range(size)])  15.7 us
    pallas_call x4, Pallas kernels, body(): pl.pallas_call(functools.partial(bulk_kernel, distance=p, first=first, pl...  8.71 us
    all_to_all x1, waiting for transfers between devices, body(): lax.all_to_all(bundle, 'ctx', split_axis=0, concat_axis=0, tiled=True, ax...  7.18 us
    pallas_call x3, Pallas kernels, split(): pl.pallas_call(functools.partial(split_kernel, seats=seats), in_specs=[sc...  6.37 us
    all_to_all x1, starting transfers between devices, body(): mix = lax.all_to_all(packed, 'ctx', split_axis=0, concat_axis=0, tiled=True)  6.1 us
    ppermute x2, starting transfers between devices, body(): arrived.append(lax.ppermute(messages[k], 'ctx', target))  4.92 us
    unnamed x23, local copies, waits for them, and re-layouts  4.15 us
  transfers between devices with their start and end apart: 17, of which 5 were waited for; matrix products, arithmetic and copies ran while one was open for 2% of the time, Pallas kernels for 18%

profile of v2, /device:TPU:0, one launch (start us, length us, event | category | flops | bytes accessed | tf_op | source)
XLA Modules:
  0.0 89.7 jit_solution(10960265299814358001)
XLA Ops:
  0.7 0.1 pad_add_fusion.place_ref
  0.7 2.5 %split.3 = (bf16[520,256]{1,0:T(8,128)(2,1)}, bf16[520,256]{1,0:T(8,128)(2,1)S(1)}) custom-call(s32[2]{0:T(128)S(1)} %pad_add_fusion.place_ref, bf16[512,1024]{1,0:T(8,128)(2,1)} %keys_ref.5, bf16[512,1024]{1,0:T(8,128)(2,1)} %values_ref.5, bf16[8,1024]{1,0:T(8,128)(2,1)} %tree_keys_ref.5, bf16[8,1024]{1,0:T(8,128)(2,1)} %tree_values_ref.5), custom_call_target="tpu_custom_call" | custom-call | flops 4000000000 | bytes 1000000 | tf_op jit(solution)/shard_map/split/pallas_call | solution.py:348
  3.2 3.1 %collective-permute-start = (bf16[520,256]{1,0:T(8,128)(2,1)}, bf16[520,256]{1,0:T(8,128)(2,1)S(1)}, u32[]{:S(2)}, u32[]{:S(2)}) collective-permute-start(bf16[520,256]{1,0:T(8,128)(2,1)} %get-tuple-element.20.refs_0_), channel_id=1, source_target_pairs={{0,4},{1,5},{2,6},{3,7},{4,0},{5,1},{6,2},{7,3},{8,12},{9,13},{10,... | collective-permute-start | bytes 798728 | tf_op jit(solution)/shard_map/ppermute | solution.py:333
  6.3 1.9 %split.4 = (bf16[520,256]{1,0:T(8,128)(2,1)S(1)}, bf16[520,256]{1,0:T(8,128)(2,1)S(1)}, bf16[520,256]{1,0:T(8,128)(2,1)S(1)}) custom-call(s32[2]{0:T(128)S(1)} %pad_add_fusion.place_ref, bf16[512,1024]{1,0:T(8,128)(2,1)} %keys_ref.5, bf16[512,1024]{1,0:T(8,128)(2,1)} %values_ref.5, bf16[8,1024]{1,0:T(8,128)(2,1)} %tree_keys_ref.5, ...), custom_call_target="tpu_custom_call" | custom-call | flops 4000000000 | bytes 1000000 | tf_op jit(solution)/shard_map/split/pallas_call | solution.py:348
  8.4 2.0 %pack.1.refs_0_ = bf16[16,8,1536]{2,1,0:T(8,128)(2,1)} custom-call(bf16[8,8192]{1,0:T(8,128)(2,1)} %query_ref.1, bf16[8,8192]{1,0:T(8,128)(2,1)} %embed_ref.1, bf16[520,256]{1,0:T(8,128)(2,1)S(1)} %get-tuple-element.21.after_ref), custom_call_target="tpu_custom_call" | custom-call | flops 4000000000 | bytes 1000000 | tf_op jit(solution)/shard_map/pack/pallas_call | solution.py:362
  10.4 6.1 %all-to-all-start = ((bf16[16,8,1536]{2,1,0:T(8,128)(2,1)}), bf16[16,8,1536]{2,1,0:T(8,128)(2,1)S(1)}, u32[]{:S(2)}, u32[]{:S(2)}) async-start(bf16[16,8,1536]{2,1,0:T(8,128)(2,1)} %pack.1.refs_0_), calls=%async_computation | async-start | bytes 786432 | tf_op jit(solution)/shard_map/all_to_all | solution.py:372
  16.5 1.9 %collective-permute-start.1 = (bf16[520,256]{1,0:T(8,128)(2,1)S(1)}, bf16[520,256]{1,0:T(8,128)(2,1)S(1)}, u32[]{:S(2)}, u32[]{:S(2)}) collective-permute-start(bf16[520,256]{1,0:T(8,128)(2,1)S(1)} %get-tuple-element.23), channel_id=1, source_target_pairs={{0,2},{1,3},{2,0},{3,1},{4,6},{5,7},{6,4},{7,5},{8,10},{9,11},{10,... | collective-permute-start | bytes 798728 | tf_op jit(solution)/shard_map/ppermute | solution.py:333
  18.4 2.4 %collective-permute-start.4 = (bf16[520,256]{1,0:T(8,128)(2,1)S(1)}, bf16[520,256]{1,0:T(8,128)(2,1)S(1)}, u32[]{:S(2)}, u32[]{:S(2)}) collective-permute-start(bf16[520,256]{1,0:T(8,128)(2,1)S(1)} %get-tuple-element.25), channel_id=1, source_target_pairs={{0,6},{1,7},{2,4},{3,5},{4,2},{5,3},{6,0},{7,1},{8,14},{9,15},{10,... | collective-permute-start | bytes 798728 | tf_op jit(solution)/shard_map/ppermute | solution.py:333
  20.8 1.9 %split.5 = (bf16[520,256]{1,0:T(8,128)(2,1)S(1)}, bf16[520,256]{1,0:T(8,128)(2,1)S(1)}, bf16[520,256]{1,0:T(8,128)(2,1)S(1)}) custom-call(s32[2]{0:T(128)S(1)} %pad_add_fusion.place_ref, bf16[512,1024]{1,0:T(8,128)(2,1)} %keys_ref.5, bf16[512,1024]{1,0:T(8,128)(2,1)} %values_ref.5, bf16[8,1024]{1,0:T(8,128)(2,1)} %tree_keys_ref.5, ...), custom_call_target="tpu_custom_call" | custom-call | flops 4000000000 | bytes 1000000 | tf_op jit(solution)/shard_map/split/pallas_call | solution.py:348
  22.8 0.7 copy-done.3
  23.5 0.2 convolution_minimum_fusion.2
  23.8 0.3 convolution_minimum_fusion
  24.1 0.1 fusion.20
  24.2 0.1 fusion.18
  24.4 0.1 broadcast_multiply_fusion
  24.5 0.1 mul.73
  24.7 0.1 multiply_reduce_fusion
  24.8 0.1 convert_element_type.46.refs_10_.pick_ref
  24.9 0.1 fusion.refs_9_
  25.0 0.2 fusion.7.refs_9_
  25.3 0.3 collective-permute-start.5
  25.6 15.9 %collective-permute-done.1.refs_2_ = bf16[520,256]{1,0:T(8,128)(2,1)S(1)} collective-permute-done((bf16[520,256]{1,0:T(8,128)(2,1)S(1)}, bf16[520,256]{1,0:T(8,128)(2,1)S(1)}, u32[]{:S(2)}, u32[]{:S(2)}) %collective-permute-start.1) | collective-permute-done | bytes 266272 | tf_op jit(solution)/shard_map/ppermute | solution.py:333
  41.5 4.5 %collective-permute-done.3.refs_4_ = bf16[520,256]{1,0:T(8,128)(2,1)S(1)} collective-permute-done((bf16[520,256]{1,0:T(8,128)(2,1)S(1)}, bf16[520,256]{1,0:T(8,128)(2,1)S(1)}, u32[]{:S(2)}, u32[]{:S(2)}) %collective-permute-start.3) | collective-permute-done | bytes 266272 | tf_op jit(solution)/shard_map/ppermute | solution.py:333
  46.1 1.4 %accepted.1 = (f32[16,640]{1,0:T(8,128)S(1)}, f32[16,640]{1,0:T(8,128)S(1)}) custom-call(s32[1]{0:T(128)} %bitcast.place_ref, bf16[128,1536]{1,0:T(8,128)(2,1)S(1)} %bitcast.44, bf16[520,256]{1,0:T(8,128)(2,1)S(1)} %get-tuple-element.22.refs_0_, bf16[520,256]{1,0:T(8,128)(2,1)S(1)} %collective-permute-done.refs_1_, ...), custom_call_target="tpu_custom_call" | custom-call | flops 4000000000 | bytes 1000000 | tf_op jit(solution)/shard_map/accepted/pallas_call | solution.py:436
  47.6 0.8 collective-permute-start.9
  48.4 4.1 %collective-permute-start.10 = (f32[16,640]{1,0:T(8,128)S(1)}, f32[16,640]{1,0:T(8,128)S(1)}, u32[]{:S(2)}, u32[]{:S(2)}) collective-permute-start(f32[16,640]{1,0:T(8,128)S(1)} %get-tuple-element.29), channel_id=1, source_target_pairs={{0,1},{1,9},{2,3},{3,11},{4,5},{5,13},{6,7},{7,15},{8,0},{9,8},{10... | collective-permute-start | bytes 122888 | tf_op jit(solution)/shard_map/ppermute | solution.py:453
  52.5 3.4 %copy-done.1 = bf16[512,8192]{1,0:T(8,128)(2,1)S(1)} copy-done((bf16[512,8192]{1,0:T(8,128)(2,1)S(1)}, bf16[512,8192]{1,0:T(8,128)(2,1)}, u32[]{:S(2)}) %copy-start.1) | copy-done | bytes 8388632
  55.9 1.3 %embed_join.1.refs_3_ = f32[16,8,1024]{2,1,0:T(8,128)S(1)} custom-call(bf16[16,128]{1,0:T(8,128)(2,1)S(1)} %convert_element_type.46.refs_10_.pick_ref, bf16[128,1536]{1,0:T(8,128)(2,1)S(1)} %bitcast.45, bf16[512,8192]{1,0:T(8,128)(2,1)S(1)} %copy-done.1), custom_call_target="tpu_custom_call" | custom-call | flops 4000000000 | bytes 1000000 | tf_op jit(solution)/shard_map/embed_join/pallas_call | solution.py:426
  57.2 1.3 %feature_join.1 = (f32[8,8,1024]{2,1,0:T(8,128)S(1)}, f32[8,8,1024]{2,1,0:T(8,128)S(1)}) custom-call(s32[1]{0:T(128)} %bitcast.11.bit_ref, f32[16,640]{1,0:T(8,128)S(1)} %collective-permute-done.9.refs_0_, f32[16,640]{1,0:T(8,128)S(1)} %collective-permute-done.10.refs_1_, bf16[512,8192]{1,0:T(8,128)(2,1)S(1)} %bitcast.43, f32[16,8,1024]{2,1,0:T(8,128)S(1)} %embed_join.1.refs_3_), custom_call_target="tpu_custom_call" | custom-call | tf_op jit(solution)/shard_map/feature_join/pallas_call | solution.py:455
  58.6 0.1 collective-permute-start.11
  58.6 2.2 %shard_map.132 = bf16[32,1152]{1,0:T(8,128)(2,1)S(1)} custom-call(s32[1]{0:T(128)} %bitcast.place_ref, bf16[128,1536]{1,0:T(8,128)(2,1)S(1)} %bitcast.46, bf16[520,256]{1,0:T(8,128)(2,1)S(1)} %get-tuple-element.22.refs_0_, bf16[520,256]{1,0:T(8,128)(2,1)S(1)} %collective-permute-done.refs_1_, bf16[520,256]{1,0:T(8,128)(2,1)S(1)} %collective-permute-done.1.refs_2_, ...), custom_call_target="tpu_custom_call" | custom-call | flops 4000000000 | bytes 1000000 | tf_op jit(solution)/shard_map/pallas_call | solution.py:480
  60.8 1.0 %collective-permute-start.7 = (bf16[32,1152]{1,0:T(8,128)(2,1)S(1)}, bf16[32,1152]{1,0:T(8,128)(2,1)S(1)}, u32[]{:S(2)}, u32[]{:S(2)}) collective-permute-start(bf16[32,1152]{1,0:T(8,128)(2,1)S(1)} %shard_map.132), channel_id=1, source_target_pairs={{0,8},{1,9},{2,10},{3,11},{4,12},{5,13},{6,14},{7,15},{8,0},{9,1},... | collective-permute-start | bytes 221192 | tf_op jit(solution)/shard_map/ppermute | solution.py:333
  61.9 0.5 collective-permute-start.12
  62.4 2.2 %shard_map.134 = bf16[32,1152]{1,0:T(8,128)(2,1)S(1)} custom-call(s32[1]{0:T(128)} %bitcast.place_ref, bf16[128,1536]{1,0:T(8,128)(2,1)S(1)} %bitcast.47, bf16[520,256]{1,0:T(8,128)(2,1)S(1)} %get-tuple-element.22.refs_0_, bf16[520,256]{1,0:T(8,128)(2,1)S(1)} %collective-permute-done.refs_1_, bf16[520,256]{1,0:T(8,128)(2,1)S(1)} %collective-permute-done.1.refs_2_, ...), custom_call_target="tpu_custom_call" | custom-call | flops 4000000000 | bytes 1000000 | tf_op jit(solution)/shard_map/pallas_call | solution.py:480
  64.6 2.4 %collective-permute-start.8 = (bf16[32,1152]{1,0:T(8,128)(2,1)S(1)}, bf16[32,1152]{1,0:T(8,128)(2,1)S(1)}, u32[]{:S(2)}, u32[]{:S(2)}) collective-permute-start(bf16[32,1152]{1,0:T(8,128)(2,1)S(1)} %shard_map.134), channel_id=1, source_target_pairs={{0,8},{1,9},{2,10},{3,11},{4,12},{5,13},{6,14},{7,15},{8,0},{9,1},... | collective-permute-start | bytes 221192 | tf_op jit(solution)/shard_map/ppermute | solution.py:333
  67.0 0.1 collective-permute-done.12.other_ref
  67.1 1.6 %collective-permute-start.13 = (f32[2,8,1024]{2,1,0:T(8,128)S(1)}, f32[2,8,1024]{2,1,0:T(8,128)S(1)}, u32[]{:S(2)}, u32[]{:S(2)}) collective-permute-start(f32[2,8,1024]{2,1,0:T(8,128)S(1)} %get-tuple-element.35), channel_id=1, source_target_pairs={{0,4},{1,5},{2,6},{3,7},{4,0},{5,1},{6,2},{7,3},{8,12},{9,13},{10,... | collective-permute-start | bytes 196616 | tf_op jit(solution)/shard_map/ppermute | solution.py:333
  68.7 2.2 %shard_map.131.refs_0_ = bf16[32,1152]{1,0:T(8,128)(2,1)S(1)} custom-call(s32[1]{0:T(128)} %bitcast.place_ref, bf16[128,1536]{1,0:T(8,128)(2,1)S(1)} %bitcast.48, bf16[520,256]{1,0:T(8,128)(2,1)S(1)} %get-tuple-element.22.refs_0_, bf16[520,256]{1,0:T(8,128)(2,1)S(1)} %collective-permute-done.refs_1_, bf16[520,256]{1,0:T(8,128)(2,1)S(1)} %collective-permute-done.1.refs_2_, ...), custom_call_target="tpu_custom_call" | custom-call | flops 4000000000 | bytes 1000000 | tf_op jit(solution)/shard_map/pallas_call | solution.py:480
  70.8 0.8 collective-permute-done.13.other_ref
  71.6 2.3 %collective-permute-start.14 = (f32[1,8,1024]{2,1,0:T(8,128)S(1)}, f32[1,8,1024]{2,1,0:T(8,128)S(1)}, u32[]{:S(2)}, u32[]{:S(2)}) collective-permute-start(f32[1,8,1024]{2,1,0:T(8,128)S(1)} %get-tuple-element.37), channel_id=1, source_target_pairs={{0,8},{1,9},{2,10},{3,11},{4,12},{5,13},{6,14},{7,15},{8,0},{9,1},... | collective-permute-start | bytes 98312 | tf_op jit(solution)/shard_map/ppermute | solution.py:333
  74.0 2.2 %shard_map.133.refs_2_ = bf16[32,1152]{1,0:T(8,128)(2,1)S(1)} custom-call(s32[1]{0:T(128)} %bitcast.place_ref, bf16[128,1536]{1,0:T(8,128)(2,1)S(1)} %bitcast.49, bf16[520,256]{1,0:T(8,128)(2,1)S(1)} %get-tuple-element.22.refs_0_, bf16[520,256]{1,0:T(8,128)(2,1)S(1)} %collective-permute-done.refs_1_, bf16[520,256]{1,0:T(8,128)(2,1)S(1)} %collective-permute-done.1.refs_2_, ...), custom_call_target="tpu_custom_call" | custom-call | flops 4000000000 | bytes 1000000 | tf_op jit(solution)/shard_map/pallas_call | solution.py:480
  76.2 0.5 merge.1.merged_ref
  76.7 0.8 bundle.1
  77.5 3.8 %all-to-all-start.1 = ((bf16[8,24,1024]{2,1,0:T(8,128)(2,1)}), bf16[8,24,1024]{2,1,0:T(8,128)(2,1)S(1)}, u32[]{:S(2)}, u32[]{:S(2)}) async-start(bf16[8,24,1024]{2,1,0:T(8,128)(2,1)} %bundle.1), calls=%async_computation.1 | async-start | bytes 786432 | tf_op jit(solution)/shard_map/all_to_all | solution.py:514
  81.3 0.1 reduce_sum.12
  81.4 0.2 fusion.19.pick_ref
  81.5 7.2 %all-to-all-done.1.bundle_ref = bf16[8,24,1024]{2,1,0:T(8,128)(2,1)S(1)} async-done(((bf16[8,24,1024]{2,1,0:T(8,128)(2,1)}), bf16[8,24,1024]{2,1,0:T(8,128)(2,1)S(1)}, u32[]{:S(2)}, u32[]{:S(2)}) %all-to-all-start.1) | async-done | bytes 393248 | tf_op jit(solution)/shard_map/all_to_all | solution.py:514
  88.7 1.0 %last.1 = (bf16[8,8192]{1,0:T(8,128)(2,1)}, bf16[8,8192]{1,0:T(8,128)(2,1)}) custom-call(bf16[8,24,1024]{2,1,0:T(8,128)(2,1)S(1)} %all-to-all-done.1.bundle_ref, f32[1,8192]{1,0:T(1,128)S(1)} %bitcast.50, f32[8,8]{1,0:T(8,128)S(1)} %fusion.19.pick_ref), custom_call_target="tpu_custom_call" | custom-call | tf_op jit(solution)/shard_map/last/pallas_call | solution.py:524
  (51 shorter events, 0.4 us)
Async XLA Ops:
  3.2 22.1 %collective-permute-start = (bf16[520,256]{1,0:T(8,128)(2,1)}, bf16[520,256]{1,0:T(8,128)(2,1)S(1)}, u32[]{:S(2)}, u32[]{:S(2)}) collective-permute-start(bf16[520,256]{1,0:T(8,128)(2,1)} %get-tuple-element.20.refs_0_), channel_id=1, source_target_pairs={{0,4},{1,5},{2,6},{3,7},{4,0},{5,1},{6,2},{7,3},{8,12},{9,13},{10,... | collective-permute-start | bytes 798728 | tf_op jit(solution)/shard_map/ppermute | solution.py:333
  8.3 33.2 %collective-permute-start.2 = (bf16[520,256]{1,0:T(8,128)(2,1)S(1)}, bf16[520,256]{1,0:T(8,128)(2,1)S(1)}, u32[]{:S(2)}, u32[]{:S(2)}) collective-permute-start(bf16[520,256]{1,0:T(8,128)(2,1)S(1)} %get-tuple-element.21.after_ref), channel_id=1, source_target_pairs={{0,5},{1,4},{2,7},{3,6},{4,1},{5,0},{6,3},{7,2},{8,13},{9,12},{10,... | collective-permute-start | bytes 798728 | tf_op jit(solution)/shard_map/ppermute | solution.py:333
  10.4 13.2 %copy-start.4 = (s32[2,64]{1,0:T(2,128)S(1)}, s32[2,64]{1,0:T(2,128)}, u32[]{:S(2)}) copy-start(s32[2,64]{1,0:T(2,128)} %param.21) | copy-start | bytes 1540
  10.4 13.6 %copy-start.5 = (s32[2]{0:T(128)S(1)}, s32[2]{0:T(128)}, u32[]{:S(2)}) copy-start(s32[2]{0:T(128)} %param.22) | copy-start | bytes 28
  10.4 35.7 %all-to-all-start = ((bf16[16,8,1536]{2,1,0:T(8,128)(2,1)}), bf16[16,8,1536]{2,1,0:T(8,128)(2,1)S(1)}, u32[]{:S(2)}, u32[]{:S(2)}) async-start(bf16[16,8,1536]{2,1,0:T(8,128)(2,1)} %pack.1.refs_0_), calls=%async_computation | async-start | bytes 786432 | tf_op jit(solution)/shard_map/all_to_all | solution.py:372
  16.5 25.0 %collective-permute-start.1 = (bf16[520,256]{1,0:T(8,128)(2,1)S(1)}, bf16[520,256]{1,0:T(8,128)(2,1)S(1)}, u32[]{:S(2)}, u32[]{:S(2)}) collective-permute-start(bf16[520,256]{1,0:T(8,128)(2,1)S(1)} %get-tuple-element.23), channel_id=1, source_target_pairs={{0,2},{1,3},{2,0},{3,1},{4,6},{5,7},{6,4},{7,5},{8,10},{9,11},{10,... | collective-permute-start | bytes 798728 | tf_op jit(solution)/shard_map/ppermute | solution.py:333
  18.4 27.6 %collective-permute-start.3 = (bf16[520,256]{1,0:T(8,128)(2,1)S(1)}, bf16[520,256]{1,0:T(8,128)(2,1)S(1)}, u32[]{:S(2)}, u32[]{:S(2)}) collective-permute-start(bf16[520,256]{1,0:T(8,128)(2,1)S(1)} %get-tuple-element.24), channel_id=1, source_target_pairs={{0,3},{1,2},{2,1},{3,0},{4,7},{5,6},{6,5},{7,4},{8,11},{9,10},{10,... | collective-permute-start | bytes 798728 | tf_op jit(solution)/shard_map/ppermute | solution.py:333
  18.4 27.6 %collective-permute-start.4 = (bf16[520,256]{1,0:T(8,128)(2,1)S(1)}, bf16[520,256]{1,0:T(8,128)(2,1)S(1)}, u32[]{:S(2)}, u32[]{:S(2)}) collective-permute-start(bf16[520,256]{1,0:T(8,128)(2,1)S(1)} %get-tuple-element.25), channel_id=1, source_target_pairs={{0,6},{1,7},{2,4},{3,5},{4,2},{5,3},{6,0},{7,1},{8,14},{9,15},{10,... | collective-permute-start | bytes 798728 | tf_op jit(solution)/shard_map/ppermute | solution.py:333
  22.8 0.7 copy-start.3
  23.5 1.8 %copy-start.2 = (bf16[520,256]{1,0:T(8,128)(2,1)}, bf16[520,256]{1,0:T(8,128)(2,1)S(1)}, u32[]{:S(2)}) copy-start(bf16[520,256]{1,0:T(8,128)(2,1)S(1)} %get-tuple-element.27) | copy-start | bytes 798724
  25.3 20.8 %collective-permute-start.5 = (bf16[520,256]{1,0:T(8,128)(2,1)}, bf16[520,256]{1,0:T(8,128)(2,1)S(1)}, u32[]{:S(2)}, u32[]{:S(2)}) collective-permute-start(bf16[520,256]{1,0:T(8,128)(2,1)} %copy-done.3), channel_id=1, source_target_pairs={{0,7},{1,6},{2,5},{3,4},{4,3},{5,2},{6,1},{7,0},{8,15},{9,14},{10,... | collective-permute-start | bytes 798728 | tf_op jit(solution)/shard_map/ppermute | solution.py:333
  41.5 4.6 %collective-permute-start.6 = (bf16[520,256]{1,0:T(8,128)(2,1)}, bf16[520,256]{1,0:T(8,128)(2,1)S(1)}, u32[]{:S(2)}, u32[]{:S(2)}) collective-permute-start(bf16[520,256]{1,0:T(8,128)(2,1)} %copy-done.2), channel_id=1, source_target_pairs={{0,1},{1,0},{2,3},{3,2},{4,5},{5,4},{6,7},{7,6},{8,9},{9,8},{10,11... | collective-permute-start | bytes 798728 | tf_op jit(solution)/shard_map/ppermute | solution.py:333
  46.1 11.1 %slice-start = ((s8[8388608]{0:T(1024)(128)(4,1)}), s8[4194304]{0:T(1024)(128)(4,1)S(1)}, s32[]{:S(2)}) async-start(s8[8388608]{0:T(1024)(128)(4,1)} %bitcast.42), calls=%async_computation.2 | async-start | bytes 8388608
  47.6 9.6 %slice-start.1 = ((s8[8388608]{0:T(1024)(128)(4,1)}), s8[4194304]{0:T(1024)(128)(4,1)S(1)}, s32[]{:S(2)}) async-start(s8[8388608]{0:T(1024)(128)(4,1)} %bitcast.42), calls=%async_computation.3 | async-start | bytes 8388608
  47.6 9.6 %collective-permute-start.9 = (f32[16,640]{1,0:T(8,128)S(1)}, f32[16,640]{1,0:T(8,128)S(1)}, u32[]{:S(2)}, u32[]{:S(2)}) collective-permute-start(f32[16,640]{1,0:T(8,128)S(1)} %get-tuple-element.28.refs_10_), channel_id=1, source_target_pairs={{0,0},{1,8},{2,2},{3,10},{4,4},{5,12},{6,6},{7,14},{8,1},{9,9},{10... | collective-permute-start | bytes 122888 | tf_op jit(solution)/shard_map/ppermute | solution.py:453
  48.4 8.8 %collective-permute-start.10 = (f32[16,640]{1,0:T(8,128)S(1)}, f32[16,640]{1,0:T(8,128)S(1)}, u32[]{:S(2)}, u32[]{:S(2)}) collective-permute-start(f32[16,640]{1,0:T(8,128)S(1)} %get-tuple-element.29), channel_id=1, source_target_pairs={{0,1},{1,9},{2,3},{3,11},{4,5},{5,13},{6,7},{7,15},{8,0},{9,8},{10... | collective-permute-start | bytes 122888 | tf_op jit(solution)/shard_map/ppermute | solution.py:453
  52.5 3.4 %copy-start.1 = (bf16[512,8192]{1,0:T(8,128)(2,1)S(1)}, bf16[512,8192]{1,0:T(8,128)(2,1)}, u32[]{:S(2)}) copy-start(bf16[512,8192]{1,0:T(8,128)(2,1)} %weight_ref.1) | copy-start | bytes 25165828
  58.6 3.3 %collective-permute-start.11 = (f32[8,8,1024]{2,1,0:T(8,128)S(1)}, f32[8,8,1024]{2,1,0:T(8,128)S(1)}, u32[]{:S(2)}, u32[]{:S(2)}) collective-permute-start(f32[8,8,1024]{2,1,0:T(8,128)S(1)} %get-tuple-element.31), channel_id=1, source_target_pairs={{0,1},{1,0},{2,3},{3,2},{4,5},{5,4},{6,7},{7,6},{8,9},{9,8},{10,11... | collective-permute-start | bytes 786440 | tf_op jit(solution)/shard_map/ppermute | solution.py:333
  60.8 15.3 %collective-permute-start.7 = (bf16[32,1152]{1,0:T(8,128)(2,1)S(1)}, bf16[32,1152]{1,0:T(8,128)(2,1)S(1)}, u32[]{:S(2)}, u32[]{:S(2)}) collective-permute-start(bf16[32,1152]{1,0:T(8,128)(2,1)S(1)} %shard_map.132), channel_id=1, source_target_pairs={{0,8},{1,9},{2,10},{3,11},{4,12},{5,13},{6,14},{7,15},{8,0},{9,1},... | collective-permute-start | bytes 221192 | tf_op jit(solution)/shard_map/ppermute | solution.py:333
  61.9 5.2 %collective-permute-start.12 = (f32[4,8,1024]{2,1,0:T(8,128)S(1)}, f32[4,8,1024]{2,1,0:T(8,128)S(1)}, u32[]{:S(2)}, u32[]{:S(2)}) collective-permute-start(f32[4,8,1024]{2,1,0:T(8,128)S(1)} %get-tuple-element.33), channel_id=1, source_target_pairs={{0,2},{1,3},{2,0},{3,1},{4,6},{5,7},{6,4},{7,5},{8,10},{9,11},{10,... | collective-permute-start | bytes 393224 | tf_op jit(solution)/shard_map/ppermute | solution.py:333
  64.6 11.6 %collective-permute-start.8 = (bf16[32,1152]{1,0:T(8,128)(2,1)S(1)}, bf16[32,1152]{1,0:T(8,128)(2,1)S(1)}, u32[]{:S(2)}, u32[]{:S(2)}) collective-permute-start(bf16[32,1152]{1,0:T(8,128)(2,1)S(1)} %shard_map.134), channel_id=1, source_target_pairs={{0,8},{1,9},{2,10},{3,11},{4,12},{5,13},{6,14},{7,15},{8,0},{9,1},... | collective-permute-start | bytes 221192 | tf_op jit(solution)/shard_map/ppermute | solution.py:333
  67.1 4.5 %collective-permute-start.13 = (f32[2,8,1024]{2,1,0:T(8,128)S(1)}, f32[2,8,1024]{2,1,0:T(8,128)S(1)}, u32[]{:S(2)}, u32[]{:S(2)}) collective-permute-start(f32[2,8,1024]{2,1,0:T(8,128)S(1)} %get-tuple-element.35), channel_id=1, source_target_pairs={{0,4},{1,5},{2,6},{3,7},{4,0},{5,1},{6,2},{7,3},{8,12},{9,13},{10,... | collective-permute-start | bytes 196616 | tf_op jit(solution)/shard_map/ppermute | solution.py:333
  71.6 17.1 %copy-start = (f32[8192]{0:T(1024)S(1)}, f32[8192]{0:T(1024)}, u32[]{:S(2)}) copy-start(f32[8192]{0:T(1024)} %param.20) | copy-start | bytes 98308
  71.6 5.1 %collective-permute-start.14 = (f32[1,8,1024]{2,1,0:T(8,128)S(1)}, f32[1,8,1024]{2,1,0:T(8,128)S(1)}, u32[]{:S(2)}, u32[]{:S(2)}) collective-permute-start(f32[1,8,1024]{2,1,0:T(8,128)S(1)} %get-tuple-element.37), channel_id=1, source_target_pairs={{0,8},{1,9},{2,10},{3,11},{4,12},{5,13},{6,14},{7,15},{8,0},{9,1},... | collective-permute-start | bytes 98312 | tf_op jit(solution)/shard_map/ppermute | solution.py:333
  77.5 11.2 %all-to-all-start.1 = ((bf16[8,24,1024]{2,1,0:T(8,128)(2,1)}), bf16[8,24,1024]{2,1,0:T(8,128)(2,1)S(1)}, u32[]{:S(2)}, u32[]{:S(2)}) async-start(bf16[8,24,1024]{2,1,0:T(8,128)(2,1)} %bundle.1), calls=%async_computation.1 | async-start | bytes 786432 | tf_op jit(solution)/shard_map/all_to_all | solution.py:514

commit v3 on v2

--- a/solution.py
+++ b/solution.py
@@ -357,8 +357,8 @@
             name="split",
         )(place, *sources, *after)
 
-    first = list(split(ARRIVAL[1:3], ()))
-    second = list(split(ARRIVAL[3:6], first[:1]))
+    first = list(split(ARRIVAL[1:4], ()))
+    second = list(split(ARRIVAL[4:7], first[:1]))
     packed = pl.pallas_call(
         functools.partial(mix_kernel, key_of=key_of),
         in_specs=[stored, stored, outside],
@@ -371,7 +371,7 @@
     )(leave(queries), leave(token_embed), second[0])
     mix = lax.all_to_all(packed, "ctx", split_axis=0, concat_axis=0, tiled=True)
     mix = pltpu.with_memory_space_constraint(mix.reshape(every_row, mixed), pltpu.VMEM)
-    third = list(split(ARRIVAL[6:] + ARRIVAL[:1], [packed]))
+    third = list(split(ARRIVAL[7:] + ARRIVAL[:1], [packed]))
     slabs = third[-1:] + first + second + third[:-1]
     for i, r in enumerate(ARRIVAL):
         if r:

time: 90.2 us -> 87.3 us (0.968)
  starting transfers between devices: 30.5 us -> 29.1 us
  waiting for transfers between devices: 28.5 us -> 27.1 us
    all_to_all x1, starting transfers between devices: 6.1 us -> 4.54 us  [body(): mix = lax.all_to_all(packed, 'ctx', split_axis=0, concat_axis=0, tiled=True)]
    ppermute x13, waiting for transfers between devices: 21.3 us -> 20 us  [swap(): return lax.ppermute(x, 'ctx', [(s, s ^ mask) for s in range(size)])]
    unnamed x23 -> x21, local copies, waits for them, and re-layouts: 4.15 us -> 3.44 us
  transfers between devices with their start and end apart: 17 -> 17, of which waited for: 5 -> 8; matrix products, arithmetic and copies ran while one was open for 2% -> 2% of each run, Pallas kernels for 18% -> 20%
where the time goes in v3:
time: 87.3 us; the launch traced here: 86.8 us
  starting transfers between devices  29.1 us (33%)
  waiting for transfers between devices  27.1 us (31%)
  Pallas kernels  24.2 us (28%)
  local copies, waits for them, and re-layouts  3.71 us (4%)
  matrix products  1.31 us (2%)
  between operations  0.97 us (1%)
    ppermute x13, waiting for transfers between devices, swap(): return lax.ppermute(x, 'ctx', [(s, s ^ mask) for s in range(size)])  20 us
    ppermute x13, starting transfers between devices, swap(): return lax.ppermute(x, 'ctx', [(s, s ^ mask) for s in range(size)])  16.1 us
    pallas_call x4, Pallas kernels, body(): pl.pallas_call(functools.partial(bulk_kernel, distance=p, first=first, pl...  8.71 us
    all_to_all x1, waiting for transfers between devices, body(): lax.all_to_all(bundle, 'ctx', split_axis=0, concat_axis=0, tiled=True, ax...  7.1 us
    pallas_call x3, Pallas kernels, split(): pl.pallas_call(functools.partial(split_kernel, seats=seats), in_specs=[sc...  7.06 us
    ppermute x2, starting transfers between devices, body(): arrived.append(lax.ppermute(messages[k], 'ctx', target))  4.93 us
    all_to_all x1, starting transfers between devices, body(): mix = lax.all_to_all(packed, 'ctx', split_axis=0, concat_axis=0, tiled=True)  4.54 us
    all_to_all x1, starting transfers between devices, body(): lax.all_to_all(bundle, 'ctx', split_axis=0, concat_axis=0, tiled=True, ax...  3.45 us
  transfers between devices with their start and end apart: 17, of which 8 were waited for; matrix products, arithmetic and copies ran while one was open for 2% of the time, Pallas kernels for 20%

profile of v3, /device:TPU:0, one launch (start us, length us, event | category | flops | bytes accessed | tf_op | source)
XLA Modules:
  0.0 86.8 jit_solution(18073850431113996650)
XLA Ops:
  0.7 2.6 %split.3 = (bf16[520,256]{1,0:T(8,128)(2,1)}, bf16[520,256]{1,0:T(8,128)(2,1)S(1)}, bf16[520,256]{1,0:T(8,128)(2,1)S(1)}) custom-call(s32[2]{0:T(128)S(1)} %pad_add_fusion.place_ref, bf16[512,1024]{1,0:T(8,128)(2,1)} %keys_ref.5, bf16[512,1024]{1,0:T(8,128)(2,1)} %values_ref.5, bf16[8,1024]{1,0:T(8,128)(2,1)} %tree_keys_ref.5, bf16[8,1024]{1,0:T(8,128)(2,1)} %tree_values_ref.5), custom_call_target="tpu_custom_call" | custom-call | flops 4000000000 | bytes 1000000 | tf_op jit(solution)/shard_map/split/pallas_call | solution.py:348
  3.4 3.1 %collective-permute-start = (bf16[520,256]{1,0:T(8,128)(2,1)}, bf16[520,256]{1,0:T(8,128)(2,1)S(1)}, u32[]{:S(2)}, u32[]{:S(2)}) collective-permute-start(bf16[520,256]{1,0:T(8,128)(2,1)} %get-tuple-element.20.refs_0_), channel_id=1, source_target_pairs={{0,4},{1,5},{2,6},{3,7},{4,0},{5,1},{6,2},{7,3},{8,12},{9,13},{10,... | collective-permute-start | bytes 798728 | tf_op jit(solution)/shard_map/ppermute | solution.py:333
  6.5 2.6 %split.4 = (bf16[520,256]{1,0:T(8,128)(2,1)}, bf16[520,256]{1,0:T(8,128)(2,1)S(1)}, bf16[520,256]{1,0:T(8,128)(2,1)S(1)}) custom-call(s32[2]{0:T(128)S(1)} %pad_add_fusion.place_ref, bf16[512,1024]{1,0:T(8,128)(2,1)} %keys_ref.5, bf16[512,1024]{1,0:T(8,128)(2,1)} %values_ref.5, bf16[8,1024]{1,0:T(8,128)(2,1)} %tree_keys_ref.5, ...), custom_call_target="tpu_custom_call" | custom-call | flops 4000000000 | bytes 1000000 | tf_op jit(solution)/shard_map/split/pallas_call | solution.py:348
  9.1 0.7 collective-permute-start.3
  9.9 2.0 %pack.1.refs_0_ = bf16[16,8,1536]{2,1,0:T(8,128)(2,1)} custom-call(bf16[8,8192]{1,0:T(8,128)(2,1)} %query_ref.1, bf16[8,8192]{1,0:T(8,128)(2,1)} %embed_ref.1, bf16[520,256]{1,0:T(8,128)(2,1)} %get-tuple-element.21.after_ref), custom_call_target="tpu_custom_call" | custom-call | flops 4000000000 | bytes 1000000 | tf_op jit(solution)/shard_map/pack/pallas_call | solution.py:362
  11.9 4.5 %all-to-all-start = ((bf16[16,8,1536]{2,1,0:T(8,128)(2,1)}), bf16[16,8,1536]{2,1,0:T(8,128)(2,1)S(1)}, u32[]{:S(2)}, u32[]{:S(2)}) async-start(bf16[16,8,1536]{2,1,0:T(8,128)(2,1)} %pack.1.refs_0_), calls=%async_computation | async-start | bytes 786432 | tf_op jit(solution)/shard_map/all_to_all | solution.py:372
  16.5 1.9 %collective-permute-start.1 = (bf16[520,256]{1,0:T(8,128)(2,1)S(1)}, bf16[520,256]{1,0:T(8,128)(2,1)S(1)}, u32[]{:S(2)}, u32[]{:S(2)}) collective-permute-start(bf16[520,256]{1,0:T(8,128)(2,1)S(1)} %get-tuple-element.23), channel_id=1, source_target_pairs={{0,2},{1,3},{2,0},{3,1},{4,6},{5,7},{6,4},{7,5},{8,10},{9,11},{10,... | collective-permute-start | bytes 798728 | tf_op jit(solution)/shard_map/ppermute | solution.py:333
  18.4 0.9 %collective-permute-start.2 = (bf16[520,256]{1,0:T(8,128)(2,1)S(1)}, bf16[520,256]{1,0:T(8,128)(2,1)S(1)}, u32[]{:S(2)}, u32[]{:S(2)}) collective-permute-start(bf16[520,256]{1,0:T(8,128)(2,1)S(1)} %get-tuple-element.24), channel_id=1, source_target_pairs={{0,5},{1,4},{2,7},{3,6},{4,1},{5,0},{6,3},{7,2},{8,13},{9,12},{10,... | collective-permute-start | bytes 798728 | tf_op jit(solution)/shard_map/ppermute | solution.py:333
  19.3 0.6 collective-permute-start.4
  19.9 1.8 %split.5 = (bf16[520,256]{1,0:T(8,128)(2,1)S(1)}, bf16[520,256]{1,0:T(8,128)(2,1)S(1)}) custom-call(s32[2]{0:T(128)S(1)} %pad_add_fusion.place_ref, bf16[512,1024]{1,0:T(8,128)(2,1)} %keys_ref.5, bf16[512,1024]{1,0:T(8,128)(2,1)} %values_ref.5, bf16[8,1024]{1,0:T(8,128)(2,1)} %tree_keys_ref.5, bf16[8,1024]{1,0:T(8,128)(2,1)} %tree_values_ref.5, ...), custom_call_target="tpu_custom_call" | custom-call | flops 4000000000 | bytes 1000000 | tf_op jit(solution)/shard_map/split/pallas_call | solution.py:348
  21.7 0.2 convolution_minimum_fusion.2
  21.9 0.3 convolution_minimum_fusion
  22.3 0.1 fusion.20
  22.4 0.1 fusion.18
  22.5 0.1 broadcast_multiply_fusion
  22.7 0.1 mul.73
  22.9 0.1 multiply_reduce_fusion
  23.0 0.1 fusion.refs_9_
  23.2 0.2 fusion.7.refs_9_
  23.5 2.4 %collective-permute-start.5 = (bf16[520,256]{1,0:T(8,128)(2,1)S(1)}, bf16[520,256]{1,0:T(8,128)(2,1)S(1)}, u32[]{:S(2)}, u32[]{:S(2)}) collective-permute-start(bf16[520,256]{1,0:T(8,128)(2,1)S(1)} %get-tuple-element.26), channel_id=1, source_target_pairs={{0,7},{1,6},{2,5},{3,4},{4,3},{5,2},{6,1},{7,0},{8,15},{9,14},{10,... | collective-permute-start | bytes 798728 | tf_op jit(solution)/shard_map/ppermute | solution.py:333
  25.9 3.6 %collective-permute-done.1.refs_2_ = bf16[520,256]{1,0:T(8,128)(2,1)S(1)} collective-permute-done((bf16[520,256]{1,0:T(8,128)(2,1)S(1)}, bf16[520,256]{1,0:T(8,128)(2,1)S(1)}, u32[]{:S(2)}, u32[]{:S(2)}) %collective-permute-start.1) | collective-permute-done | bytes 266272 | tf_op jit(solution)/shard_map/ppermute | solution.py:333
  29.5 1.5 %collective-permute-done.2.refs_3_ = bf16[520,256]{1,0:T(8,128)(2,1)S(1)} collective-permute-done((bf16[520,256]{1,0:T(8,128)(2,1)S(1)}, bf16[520,256]{1,0:T(8,128)(2,1)S(1)}, u32[]{:S(2)}, u32[]{:S(2)}) %collective-permute-start.2) | collective-permute-done | bytes 266272 | tf_op jit(solution)/shard_map/ppermute | solution.py:333
  31.0 7.7 %collective-permute-done.4.refs_5_ = bf16[520,256]{1,0:T(8,128)(2,1)S(1)} collective-permute-done((bf16[520,256]{1,0:T(8,128)(2,1)S(1)}, bf16[520,256]{1,0:T(8,128)(2,1)S(1)}, u32[]{:S(2)}, u32[]{:S(2)}) %collective-permute-start.4) | collective-permute-done | bytes 266272 | tf_op jit(solution)/shard_map/ppermute | solution.py:333
  38.8 4.6 %collective-permute-done.5.refs_6_ = bf16[520,256]{1,0:T(8,128)(2,1)S(1)} collective-permute-done((bf16[520,256]{1,0:T(8,128)(2,1)S(1)}, bf16[520,256]{1,0:T(8,128)(2,1)S(1)}, u32[]{:S(2)}, u32[]{:S(2)}) %collective-permute-start.5) | collective-permute-done | bytes 266272 | tf_op jit(solution)/shard_map/ppermute | solution.py:333
  43.4 1.4 %accepted.1 = (f32[16,640]{1,0:T(8,128)S(1)}, f32[16,640]{1,0:T(8,128)S(1)}) custom-call(s32[1]{0:T(128)} %bitcast.place_ref, bf16[128,1536]{1,0:T(8,128)(2,1)S(1)} %bitcast.44, bf16[520,256]{1,0:T(8,128)(2,1)S(1)} %get-tuple-element.22.refs_0_, bf16[520,256]{1,0:T(8,128)(2,1)S(1)} %collective-permute-done.refs_1_, ...), custom_call_target="tpu_custom_call" | custom-call | flops 4000000000 | bytes 1000000 | tf_op jit(solution)/shard_map/accepted/pallas_call | solution.py:436
  44.8 0.8 collective-permute-start.9
  45.6 4.1 %collective-permute-start.10 = (f32[16,640]{1,0:T(8,128)S(1)}, f32[16,640]{1,0:T(8,128)S(1)}, u32[]{:S(2)}, u32[]{:S(2)}) collective-permute-start(f32[16,640]{1,0:T(8,128)S(1)} %get-tuple-element.29), channel_id=1, source_target_pairs={{0,1},{1,9},{2,3},{3,11},{4,5},{5,13},{6,7},{7,15},{8,0},{9,8},{10... | collective-permute-start | bytes 122888 | tf_op jit(solution)/shard_map/ppermute | solution.py:453
  49.8 3.4 %copy-done.1 = bf16[512,8192]{1,0:T(8,128)(2,1)S(1)} copy-done((bf16[512,8192]{1,0:T(8,128)(2,1)S(1)}, bf16[512,8192]{1,0:T(8,128)(2,1)}, u32[]{:S(2)}) %copy-start.1) | copy-done | bytes 8388632
  53.2 1.3 %embed_join.1.refs_3_ = f32[16,8,1024]{2,1,0:T(8,128)S(1)} custom-call(bf16[16,128]{1,0:T(8,128)(2,1)S(1)} %convert_element_type.46.refs_10_.pick_ref, bf16[128,1536]{1,0:T(8,128)(2,1)S(1)} %bitcast.45, bf16[512,8192]{1,0:T(8,128)(2,1)S(1)} %copy-done.1), custom_call_target="tpu_custom_call" | custom-call | flops 4000000000 | bytes 1000000 | tf_op jit(solution)/shard_map/embed_join/pallas_call | solution.py:426
  54.5 1.3 %feature_join.1 = (f32[8,8,1024]{2,1,0:T(8,128)S(1)}, f32[8,8,1024]{2,1,0:T(8,128)S(1)}) custom-call(s32[1]{0:T(128)} %bitcast.11.bit_ref, f32[16,640]{1,0:T(8,128)S(1)} %collective-permute-done.9.refs_0_, f32[16,640]{1,0:T(8,128)S(1)} %collective-permute-done.10.refs_1_, bf16[512,8192]{1,0:T(8,128)(2,1)S(1)} %bitcast.43, f32[16,8,1024]{2,1,0:T(8,128)S(1)} %embed_join.1.refs_3_), custom_call_target="tpu_custom_call" | custom-call | tf_op jit(solution)/shard_map/feature_join/pallas_call | solution.py:455
  55.9 2.2 %shard_map.132 = bf16[32,1152]{1,0:T(8,128)(2,1)S(1)} custom-call(s32[1]{0:T(128)} %bitcast.place_ref, bf16[128,1536]{1,0:T(8,128)(2,1)S(1)} %bitcast.46, bf16[520,256]{1,0:T(8,128)(2,1)S(1)} %get-tuple-element.22.refs_0_, bf16[520,256]{1,0:T(8,128)(2,1)S(1)} %collective-permute-done.refs_1_, bf16[520,256]{1,0:T(8,128)(2,1)S(1)} %collective-permute-done.1.refs_2_, ...), custom_call_target="tpu_custom_call" | custom-call | flops 4000000000 | bytes 1000000 | tf_op jit(solution)/shard_map/pallas_call | solution.py:480
  58.1 1.0 %collective-permute-start.7 = (bf16[32,1152]{1,0:T(8,128)(2,1)S(1)}, bf16[32,1152]{1,0:T(8,128)(2,1)S(1)}, u32[]{:S(2)}, u32[]{:S(2)}) collective-permute-start(bf16[32,1152]{1,0:T(8,128)(2,1)S(1)} %shard_map.132), channel_id=1, source_target_pairs={{0,8},{1,9},{2,10},{3,11},{4,12},{5,13},{6,14},{7,15},{8,0},{9,1},... | collective-permute-start | bytes 221192 | tf_op jit(solution)/shard_map/ppermute | solution.py:333
  59.1 0.6 collective-permute-start.12
  59.7 2.2 %shard_map.134 = bf16[32,1152]{1,0:T(8,128)(2,1)S(1)} custom-call(s32[1]{0:T(128)} %bitcast.place_ref, bf16[128,1536]{1,0:T(8,128)(2,1)S(1)} %bitcast.47, bf16[520,256]{1,0:T(8,128)(2,1)S(1)} %get-tuple-element.22.refs_0_, bf16[520,256]{1,0:T(8,128)(2,1)S(1)} %collective-permute-done.refs_1_, bf16[520,256]{1,0:T(8,128)(2,1)S(1)} %collective-permute-done.1.refs_2_, ...), custom_call_target="tpu_custom_call" | custom-call | flops 4000000000 | bytes 1000000 | tf_op jit(solution)/shard_map/pallas_call | solution.py:480
  61.9 2.1 %collective-permute-start.8 = (bf16[32,1152]{1,0:T(8,128)(2,1)S(1)}, bf16[32,1152]{1,0:T(8,128)(2,1)S(1)}, u32[]{:S(2)}, u32[]{:S(2)}) collective-permute-start(bf16[32,1152]{1,0:T(8,128)(2,1)S(1)} %shard_map.134), channel_id=1, source_target_pairs={{0,8},{1,9},{2,10},{3,11},{4,12},{5,13},{6,14},{7,15},{8,0},{9,1},... | collective-permute-start | bytes 221192 | tf_op jit(solution)/shard_map/ppermute | solution.py:333
  64.0 0.3 collective-permute-done.12.other_ref
  64.3 0.6 collective-permute-start.13
  64.9 2.2 %shard_map.131.refs_0_ = bf16[32,1152]{1,0:T(8,128)(2,1)S(1)} custom-call(s32[1]{0:T(128)} %bitcast.place_ref, bf16[128,1536]{1,0:T(8,128)(2,1)S(1)} %bitcast.48, bf16[520,256]{1,0:T(8,128)(2,1)S(1)} %get-tuple-element.22.refs_0_, bf16[520,256]{1,0:T(8,128)(2,1)S(1)} %collective-permute-done.refs_1_, bf16[520,256]{1,0:T(8,128)(2,1)S(1)} %collective-permute-done.1.refs_2_, ...), custom_call_target="tpu_custom_call" | custom-call | flops 4000000000 | bytes 1000000 | tf_op jit(solution)/shard_map/pallas_call | solution.py:480
  67.1 2.0 %collective-permute-done.13.other_ref = f32[2,8,1024]{2,1,0:T(8,128)S(1)} collective-permute-done((f32[2,8,1024]{2,1,0:T(8,128)S(1)}, f32[2,8,1024]{2,1,0:T(8,128)S(1)}, u32[]{:S(2)}, u32[]{:S(2)}) %collective-permute-start.13) | collective-permute-done | bytes 65568 | tf_op jit(solution)/shard_map/ppermute | solution.py:333
  69.2 2.0 %collective-permute-start.14 = (f32[1,8,1024]{2,1,0:T(8,128)S(1)}, f32[1,8,1024]{2,1,0:T(8,128)S(1)}, u32[]{:S(2)}, u32[]{:S(2)}) collective-permute-start(f32[1,8,1024]{2,1,0:T(8,128)S(1)} %get-tuple-element.37), channel_id=1, source_target_pairs={{0,8},{1,9},{2,10},{3,11},{4,12},{5,13},{6,14},{7,15},{8,0},{9,1},... | collective-permute-start | bytes 98312 | tf_op jit(solution)/shard_map/ppermute | solution.py:333
  71.2 2.2 %shard_map.133.refs_2_ = bf16[32,1152]{1,0:T(8,128)(2,1)S(1)} custom-call(s32[1]{0:T(128)} %bitcast.place_ref, bf16[128,1536]{1,0:T(8,128)(2,1)S(1)} %bitcast.49, bf16[520,256]{1,0:T(8,128)(2,1)S(1)} %get-tuple-element.22.refs_0_, bf16[520,256]{1,0:T(8,128)(2,1)S(1)} %collective-permute-done.refs_1_, bf16[520,256]{1,0:T(8,128)(2,1)S(1)} %collective-permute-done.1.refs_2_, ...), custom_call_target="tpu_custom_call" | custom-call | flops 4000000000 | bytes 1000000 | tf_op jit(solution)/shard_map/pallas_call | solution.py:480
  73.4 0.5 merge.1.merged_ref
  73.9 0.2 collective-permute-done.14.other_ref
  74.2 0.8 bundle.1
  74.9 3.5 %all-to-all-start.1 = ((bf16[8,24,1024]{2,1,0:T(8,128)(2,1)}), bf16[8,24,1024]{2,1,0:T(8,128)(2,1)S(1)}, u32[]{:S(2)}, u32[]{:S(2)}) async-start(bf16[8,24,1024]{2,1,0:T(8,128)(2,1)} %bundle.1), calls=%async_computation.1 | async-start | bytes 786432 | tf_op jit(solution)/shard_map/all_to_all | solution.py:514
  78.5 0.2 fusion.19.pick_ref
  78.7 7.1 %all-to-all-done.1.bundle_ref = bf16[8,24,1024]{2,1,0:T(8,128)(2,1)S(1)} async-done(((bf16[8,24,1024]{2,1,0:T(8,128)(2,1)}), bf16[8,24,1024]{2,1,0:T(8,128)(2,1)S(1)}, u32[]{:S(2)}, u32[]{:S(2)}) %all-to-all-start.1) | async-done | bytes 393248 | tf_op jit(solution)/shard_map/all_to_all | solution.py:514
  85.8 1.0 %last.1 = (bf16[8,8192]{1,0:T(8,128)(2,1)}, bf16[8,8192]{1,0:T(8,128)(2,1)}) custom-call(bf16[8,24,1024]{2,1,0:T(8,128)(2,1)S(1)} %all-to-all-done.1.bundle_ref, f32[1,8192]{1,0:T(1,128)S(1)} %bitcast.50, f32[8,8]{1,0:T(8,128)S(1)} %fusion.19.pick_ref), custom_call_target="tpu_custom_call" | custom-call | tf_op jit(solution)/shard_map/last/pallas_call | solution.py:524
  (49 shorter events, 0.7 us)
Async XLA Ops:
  3.4 20.1 %collective-permute-start = (bf16[520,256]{1,0:T(8,128)(2,1)}, bf16[520,256]{1,0:T(8,128)(2,1)S(1)}, u32[]{:S(2)}, u32[]{:S(2)}) collective-permute-start(bf16[520,256]{1,0:T(8,128)(2,1)} %get-tuple-element.20.refs_0_), channel_id=1, source_target_pairs={{0,4},{1,5},{2,6},{3,7},{4,0},{5,1},{6,2},{7,3},{8,12},{9,13},{10,... | collective-permute-start | bytes 798728 | tf_op jit(solution)/shard_map/ppermute | solution.py:333
  9.1 21.9 %collective-permute-start.3 = (bf16[520,256]{1,0:T(8,128)(2,1)}, bf16[520,256]{1,0:T(8,128)(2,1)S(1)}, u32[]{:S(2)}, u32[]{:S(2)}) collective-permute-start(bf16[520,256]{1,0:T(8,128)(2,1)} %get-tuple-element.21.after_ref), channel_id=1, source_target_pairs={{0,3},{1,2},{2,1},{3,0},{4,7},{5,6},{6,5},{7,4},{8,11},{9,10},{10,... | collective-permute-start | bytes 798728 | tf_op jit(solution)/shard_map/ppermute | solution.py:333
  11.9 9.8 %copy-start.3 = (s32[2,64]{1,0:T(2,128)S(1)}, s32[2,64]{1,0:T(2,128)}, u32[]{:S(2)}) copy-start(s32[2,64]{1,0:T(2,128)} %param.21) | copy-start | bytes 1540
  11.9 10.3 %copy-start.4 = (s32[2]{0:T(128)S(1)}, s32[2]{0:T(128)}, u32[]{:S(2)}) copy-start(s32[2]{0:T(128)} %param.22) | copy-start | bytes 28
  11.9 31.4 %all-to-all-start = ((bf16[16,8,1536]{2,1,0:T(8,128)(2,1)}), bf16[16,8,1536]{2,1,0:T(8,128)(2,1)S(1)}, u32[]{:S(2)}, u32[]{:S(2)}) async-start(bf16[16,8,1536]{2,1,0:T(8,128)(2,1)} %pack.1.refs_0_), calls=%async_computation | async-start | bytes 786432 | tf_op jit(solution)/shard_map/all_to_all | solution.py:372
  16.5 13.0 %collective-permute-start.1 = (bf16[520,256]{1,0:T(8,128)(2,1)S(1)}, bf16[520,256]{1,0:T(8,128)(2,1)S(1)}, u32[]{:S(2)}, u32[]{:S(2)}) collective-permute-start(bf16[520,256]{1,0:T(8,128)(2,1)S(1)} %get-tuple-element.23), channel_id=1, source_target_pairs={{0,2},{1,3},{2,0},{3,1},{4,6},{5,7},{6,4},{7,5},{8,10},{9,11},{10,... | collective-permute-start | bytes 798728 | tf_op jit(solution)/shard_map/ppermute | solution.py:333
  18.4 12.6 %collective-permute-start.2 = (bf16[520,256]{1,0:T(8,128)(2,1)S(1)}, bf16[520,256]{1,0:T(8,128)(2,1)S(1)}, u32[]{:S(2)}, u32[]{:S(2)}) collective-permute-start(bf16[520,256]{1,0:T(8,128)(2,1)S(1)} %get-tuple-element.24), channel_id=1, source_target_pairs={{0,5},{1,4},{2,7},{3,6},{4,1},{5,0},{6,3},{7,2},{8,13},{9,12},{10,... | collective-permute-start | bytes 798728 | tf_op jit(solution)/shard_map/ppermute | solution.py:333
  19.3 19.5 %collective-permute-start.4 = (bf16[520,256]{1,0:T(8,128)(2,1)S(1)}, bf16[520,256]{1,0:T(8,128)(2,1)S(1)}, u32[]{:S(2)}, u32[]{:S(2)}) collective-permute-start(bf16[520,256]{1,0:T(8,128)(2,1)S(1)} %get-tuple-element.25), channel_id=1, source_target_pairs={{0,6},{1,7},{2,4},{3,5},{4,2},{5,3},{6,0},{7,1},{8,14},{9,15},{10,... | collective-permute-start | bytes 798728 | tf_op jit(solution)/shard_map/ppermute | solution.py:333
  21.6 1.8 %copy-start.2 = (bf16[520,256]{1,0:T(8,128)(2,1)}, bf16[520,256]{1,0:T(8,128)(2,1)S(1)}, u32[]{:S(2)}) copy-start(bf16[520,256]{1,0:T(8,128)(2,1)S(1)} %get-tuple-element.27) | copy-start | bytes 798724
  23.5 19.9 %collective-permute-start.5 = (bf16[520,256]{1,0:T(8,128)(2,1)S(1)}, bf16[520,256]{1,0:T(8,128)(2,1)S(1)}, u32[]{:S(2)}, u32[]{:S(2)}) collective-permute-start(bf16[520,256]{1,0:T(8,128)(2,1)S(1)} %get-tuple-element.26), channel_id=1, source_target_pairs={{0,7},{1,6},{2,5},{3,4},{4,3},{5,2},{6,1},{7,0},{8,15},{9,14},{10,... | collective-permute-start | bytes 798728 | tf_op jit(solution)/shard_map/ppermute | solution.py:333
  29.5 13.8 %collective-permute-start.6 = (bf16[520,256]{1,0:T(8,128)(2,1)}, bf16[520,256]{1,0:T(8,128)(2,1)S(1)}, u32[]{:S(2)}, u32[]{:S(2)}) collective-permute-start(bf16[520,256]{1,0:T(8,128)(2,1)} %copy-done.2), channel_id=1, source_target_pairs={{0,1},{1,0},{2,3},{3,2},{4,5},{5,4},{6,7},{7,6},{8,9},{9,8},{10,11... | collective-permute-start | bytes 798728 | tf_op jit(solution)/shard_map/ppermute | solution.py:333
  43.4 11.1 %slice-start = ((s8[8388608]{0:T(1024)(128)(4,1)}), s8[4194304]{0:T(1024)(128)(4,1)S(1)}, s32[]{:S(2)}) async-start(s8[8388608]{0:T(1024)(128)(4,1)} %bitcast.42), calls=%async_computation.2 | async-start | bytes 8388608
  44.8 9.7 %slice-start.1 = ((s8[8388608]{0:T(1024)(128)(4,1)}), s8[4194304]{0:T(1024)(128)(4,1)S(1)}, s32[]{:S(2)}) async-start(s8[8388608]{0:T(1024)(128)(4,1)} %bitcast.42), calls=%async_computation.3 | async-start | bytes 8388608
  44.8 9.6 %collective-permute-start.9 = (f32[16,640]{1,0:T(8,128)S(1)}, f32[16,640]{1,0:T(8,128)S(1)}, u32[]{:S(2)}, u32[]{:S(2)}) collective-permute-start(f32[16,640]{1,0:T(8,128)S(1)} %get-tuple-element.28.refs_10_), channel_id=1, source_target_pairs={{0,0},{1,8},{2,2},{3,10},{4,4},{5,12},{6,6},{7,14},{8,1},{9,9},{10... | collective-permute-start | bytes 122888 | tf_op jit(solution)/shard_map/ppermute | solution.py:453
  45.6 8.8 %collective-permute-start.10 = (f32[16,640]{1,0:T(8,128)S(1)}, f32[16,640]{1,0:T(8,128)S(1)}, u32[]{:S(2)}, u32[]{:S(2)}) collective-permute-start(f32[16,640]{1,0:T(8,128)S(1)} %get-tuple-element.29), channel_id=1, source_target_pairs={{0,1},{1,9},{2,3},{3,11},{4,5},{5,13},{6,7},{7,15},{8,0},{9,8},{10... | collective-permute-start | bytes 122888 | tf_op jit(solution)/shard_map/ppermute | solution.py:453
  49.8 3.4 %copy-start.1 = (bf16[512,8192]{1,0:T(8,128)(2,1)S(1)}, bf16[512,8192]{1,0:T(8,128)(2,1)}, u32[]{:S(2)}) copy-start(bf16[512,8192]{1,0:T(8,128)(2,1)} %weight_ref.1) | copy-start | bytes 25165828
  55.8 3.2 %collective-permute-start.11 = (f32[8,8,1024]{2,1,0:T(8,128)S(1)}, f32[8,8,1024]{2,1,0:T(8,128)S(1)}, u32[]{:S(2)}, u32[]{:S(2)}) collective-permute-start(f32[8,8,1024]{2,1,0:T(8,128)S(1)} %get-tuple-element.31), channel_id=1, source_target_pairs={{0,1},{1,0},{2,3},{3,2},{4,5},{5,4},{6,7},{7,6},{8,9},{9,8},{10,11... | collective-permute-start | bytes 786440 | tf_op jit(solution)/shard_map/ppermute | solution.py:333
  58.1 15.3 %collective-permute-start.7 = (bf16[32,1152]{1,0:T(8,128)(2,1)S(1)}, bf16[32,1152]{1,0:T(8,128)(2,1)S(1)}, u32[]{:S(2)}, u32[]{:S(2)}) collective-permute-start(bf16[32,1152]{1,0:T(8,128)(2,1)S(1)} %shard_map.132), channel_id=1, source_target_pairs={{0,8},{1,9},{2,10},{3,11},{4,12},{5,13},{6,14},{7,15},{8,0},{9,1},... | collective-permute-start | bytes 221192 | tf_op jit(solution)/shard_map/ppermute | solution.py:333
  59.1 5.2 %collective-permute-start.12 = (f32[4,8,1024]{2,1,0:T(8,128)S(1)}, f32[4,8,1024]{2,1,0:T(8,128)S(1)}, u32[]{:S(2)}, u32[]{:S(2)}) collective-permute-start(f32[4,8,1024]{2,1,0:T(8,128)S(1)} %get-tuple-element.33), channel_id=1, source_target_pairs={{0,2},{1,3},{2,0},{3,1},{4,6},{5,7},{6,4},{7,5},{8,10},{9,11},{10,... | collective-permute-start | bytes 393224 | tf_op jit(solution)/shard_map/ppermute | solution.py:333
  61.9 11.5 %collective-permute-start.8 = (bf16[32,1152]{1,0:T(8,128)(2,1)S(1)}, bf16[32,1152]{1,0:T(8,128)(2,1)S(1)}, u32[]{:S(2)}, u32[]{:S(2)}) collective-permute-start(bf16[32,1152]{1,0:T(8,128)(2,1)S(1)} %shard_map.134), channel_id=1, source_target_pairs={{0,8},{1,9},{2,10},{3,11},{4,12},{5,13},{6,14},{7,15},{8,0},{9,1},... | collective-permute-start | bytes 221192 | tf_op jit(solution)/shard_map/ppermute | solution.py:333
  64.3 4.9 %collective-permute-start.13 = (f32[2,8,1024]{2,1,0:T(8,128)S(1)}, f32[2,8,1024]{2,1,0:T(8,128)S(1)}, u32[]{:S(2)}, u32[]{:S(2)}) collective-permute-start(f32[2,8,1024]{2,1,0:T(8,128)S(1)} %get-tuple-element.35), channel_id=1, source_target_pairs={{0,4},{1,5},{2,6},{3,7},{4,0},{5,1},{6,2},{7,3},{8,12},{9,13},{10,... | collective-permute-start | bytes 196616 | tf_op jit(solution)/shard_map/ppermute | solution.py:333
  69.1 16.6 %copy-start = (f32[8192]{0:T(1024)S(1)}, f32[8192]{0:T(1024)}, u32[]{:S(2)}) copy-start(f32[8192]{0:T(1024)} %param.20) | copy-start | bytes 98308
  69.2 5.0 %collective-permute-start.14 = (f32[1,8,1024]{2,1,0:T(8,128)S(1)}, f32[1,8,1024]{2,1,0:T(8,128)S(1)}, u32[]{:S(2)}, u32[]{:S(2)}) collective-permute-start(f32[1,8,1024]{2,1,0:T(8,128)S(1)} %get-tuple-element.37), channel_id=1, source_target_pairs={{0,8},{1,9},{2,10},{3,11},{4,12},{5,13},{6,14},{7,15},{8,0},{9,1},... | collective-permute-start | bytes 98312 | tf_op jit(solution)/shard_map/ppermute | solution.py:333
  74.9 10.8 %all-to-all-start.1 = ((bf16[8,24,1024]{2,1,0:T(8,128)(2,1)}), bf16[8,24,1024]{2,1,0:T(8,128)(2,1)S(1)}, u32[]{:S(2)}, u32[]{:S(2)}) async-start(bf16[8,24,1024]{2,1,0:T(8,128)(2,1)} %bundle.1), calls=%async_computation.1 | async-start | bytes 786432 | tf_op jit(solution)/shard_map/all_to_all | solution.py:514
